TPU v7x, 32 devices: a whole 2x2x4 slice. The times are simulated.
32 devices in a mesh: expert: 8 (over y, x, core), tensor: 4 (over z).
Axes of the slice: x: 2, y: 2, z: 4, core: 2. Of those that a mesh axis runs over, the one named last changes fastest.
Arguments:
- tokens: bfloat16 [512, 4096], P('expert', 'tensor'), may hold values from -6 to 6
- expert_ids: int32 [512, 8], P('expert'), may hold values from 0 to 7, all different within a row; in each aligned block of 64 rows (0 to 63, 64 to 127, ...) at most 64 rows name the same one
- gate_weights: float32 [512, 8], P('expert'), may hold values from 0.1 to 1
- w_gate: bfloat16 [8, 4096, 1536], P('expert', None, 'tensor'), may hold values from -0.09375 to 0.09375
- w_up: bfloat16 [8, 4096, 1536], P('expert', None, 'tensor'), may hold values from -0.09375 to 0.09375
- w_down: bfloat16 [8, 1536, 4096], P('expert', 'tensor'), may hold values from -0.15625 to 0.15625
Outputs:
- mixed: bfloat16 [512, 4096], P('expert', 'tensor')
Inputs may be any that keep to these rules, and one draw needn't show every extreme that they name: `expert_ids`: each row names 8 different experts. Within each aligned block of 64 rows no expert is named by more than 64 rows, and in every draw some expert is named by exactly 64 rows of some block.
All inputs are finite; a program needn't handle non-finite values.
Results may differ from a plain program's by a relative error of at most 0.02.
Values may be sent and summed in bfloat16 or wider, within the bound.
No kernel may reach another device: no remote copies, remote signals or barrier semaphores. Data moves between devices by JAX's collectives and lax.ppermute only.
A program may use at most 64 MiB of HBM per device.

v0:
```python
import jax
import jax.numpy as jnp
from jax import lax
from jax.sharding import PartitionSpec as P


def local(tokens, expert_ids, gate_weights, w_gate, w_up, w_down):
    experts = lax.axis_size("expert")
    tok_rows, top_count = expert_ids.shape
    capacity = min(tok_rows, 3 * tok_rows * top_count // (2 * experts))
    slots_all = experts * capacity
    flat_ids = expert_ids.reshape(-1)
    onehot = (flat_ids[:, None] == jnp.arange(experts, dtype=jnp.int32)[None, :]).astype(jnp.int32)
    slot_rank = jnp.sum((jnp.cumsum(onehot, axis=0) - onehot) * onehot, axis=1)
    places = (flat_ids * capacity + slot_rank).reshape(tok_rows, top_count)
    slot_range = jnp.arange(slots_all, dtype=jnp.int32)[None, :]
    selector = jnp.zeros((tok_rows, slots_all), jnp.float32)
    combine_weights = jnp.zeros((tok_rows, slots_all), jnp.float32)
    for choice_index in range(top_count):
        hit = places[:, choice_index][:, None] == slot_range
        selector = selector + hit.astype(jnp.float32)
        combine_weights = combine_weights + jnp.where(
            hit, gate_weights[:, choice_index][:, None], 0.0
        )
    selector = selector.astype(jnp.bfloat16)
    outgoing = lax.dot_general(
        selector, tokens, (((0,), (0,)), ((), ())), preferred_element_type=jnp.float32
    ).astype(jnp.bfloat16)
    arrived = lax.all_to_all(outgoing, "expert", split_axis=0, concat_axis=0, tiled=True)
    hidden_units = w_gate.shape[2]
    paired = jnp.concatenate([w_gate[0], w_up[0]], axis=1)
    gate_up = jnp.dot(
        lax.all_gather(arrived, "tensor", axis=1, tiled=True),
        paired,
        preferred_element_type=jnp.float32,
    )
    hidden = (jax.nn.silu(gate_up[:, :hidden_units]) * gate_up[:, hidden_units:]).astype(
        jnp.bfloat16
    )
    down_rows = w_down[0]
    summed = lax.psum_scatter(
        lax.dot_general(
            down_rows, hidden, (((0,), (1,)), ((), ())), preferred_element_type=jnp.float32
        ).astype(jnp.bfloat16),
        "tensor",
        scatter_dimension=0,
        tiled=True,
    )
    returned = lax.all_to_all(summed, "expert", split_axis=1, concat_axis=1, tiled=True)
    mixed = lax.dot_general(
        combine_weights,
        returned.astype(jnp.float32),
        (((1,), (1,)), ((), ())),
        precision=lax.Precision.HIGHEST,
        preferred_element_type=jnp.float32,
    )
    return mixed.astype(jnp.bfloat16)


def solution(mesh):
    placed = (
        P("expert", "tensor"),
        P("expert", None),
        P("expert", None),
        P("expert", None, "tensor"),
        P("expert", None, "tensor"),
        P("expert", "tensor", None),
    )
    return jax.shard_map(
        local, mesh=mesh, in_specs=placed, out_specs=P("expert", "tensor"), check_vma=False
    )
```

profile of v0, /device:TPU:0, one launch (start us, length us, event | category | flops | bytes accessed | tf_op | source)
XLA Modules:
  0.0 228.7 jit_solution(7367003493673571941)
XLA Ops:
  6.5 0.0 copy-start
  6.5 0.0 all-gather.2.cloned.1.call-start
  6.5 0.9 copy.15
  7.5 0.1 eq.149
  7.6 0.1 eq.145
  7.7 1.1 reduce-window.6
  8.8 0.2 slice_reduce_fusion
  9.1 0.1 fusion.50
  9.2 0.1 reduce_sum.12
  9.2 0.1 copy.17
  9.3 0.7 multiply_add_fusion
  10.0 1.5 convolution_convert_fusion.1
  11.6 20.4 %all_to_all.24 = bf16[8,64,1024]{2,1,0:T(8,128)(2,1)} all-to-all(bf16[8,64,1024]{2,1,0:T(8,128)(2,1)S(1)} %bitcast.55), channel_id=1, replica_groups=mesh['expert'=8,'tensor'=4] {'expert'}, dimensions={0} | all-to-all | bytes 2097152 | tf_op jit(solution)/shard_map/all_to_all | solution.py:29
  32.0 0.0 all-gather.2.cloned.1.call-update
  32.0 0.0 reduce-scatter.2.cloned.1.call-start
  32.1 80.2 %all-gather.2.cloned.1.call-done = bf16[512,4096]{1,0:T(8,128)(2,1)} async-done(((bf16[512,1024]{1,0:T(8,128)(2,1)}), bf16[512,4096]{1,0:T(8,128)(2,1)}) %all-gather.2.cloned.1.call-update) | async-done | bytes 4194320 | tf_op jit(solution)/shard_map/all_gather | solution.py:33
  112.3 7.5 %fusion = f32[512,768]{1,0:T(8,128)S(1)} fusion(bf16[512,4096]{1,0:T(8,128)(2,1)} %all-gather.2.cloned.1.call-done, bf16[4096,384]{1,0:T(8,128)(2,1)} %bitcast.57, bf16[4096,384]{1,0:T(8,128)(2,1)} %bitcast.58), kind=kOutput, calls=%fused_computation | convolution fusion | flops 3233808384 | bytes 12058624 | tf_op jit(solution)/shard_map/dot_general | solution.py:32
  119.7 0.0 copy-done
  119.7 4.3 %fusion.4 = bf16[4096,512]{0,1:T(8,128)(2,1)} fusion(bf16[1,384,4096]{2,1,0:T(8,128)(2,1)S(1)} %copy-done, f32[512,768]{1,0:T(8,128)S(1)} %fusion), kind=kOutput, calls=%fused_computation.5 | convolution fusion | flops 1613889536 | bytes 8912896 | tf_op jit(solution)/shard_map/dot_general | solution.py:42
  124.1 0.0 reduce-scatter.2.cloned.1.call-update
  124.1 75.4 %reduce-scatter.2.cloned.1.call-done = bf16[1024,512]{0,1:T(8,128)(2,1)} async-done(((bf16[4096,512]{0,1:T(8,128)(2,1)}), bf16[1024,512]{0,1:T(8,128)(2,1)}) %reduce-scatter.2.cloned.1.call-update) | async-done | bytes 1048592 | tf_op jit(solution)/shard_map/reduce_scatter | solution.py:41
  199.5 4.2 %all-to-all-start.1 = ((bf16[1024,8,64]{0,2,1:T(8,128)(2,1)}), bf16[1024,8,64]{0,2,1:T(8,128)(2,1)}, u32[]{:S(2)}, u32[]{:S(2)}) async-start(bf16[1024,8,64]{0,2,1:T(8,128)(2,1)} %bitcast.56), calls=%async_computation.2 | async-start | bytes 2097152 | tf_op jit(solution)/shard_map/all_to_all | solution.py:49
  203.8 15.4 %all-to-all-done.1 = bf16[1024,8,64]{0,2,1:T(8,128)(2,1)} async-done(((bf16[1024,8,64]{0,2,1:T(8,128)(2,1)}), bf16[1024,8,64]{0,2,1:T(8,128)(2,1)}, u32[]{:S(2)}, u32[]{:S(2)}) %all-to-all-start.1) | async-done | bytes 1048608 | tf_op jit(solution)/shard_map/all_to_all | solution.py:49
  219.1 2.7 %convolution_convert_fusion.2 = bf16[64,1024]{1,0:T(8,128)(2,1)} fusion(bf16[1024,512]{0,1:T(8,128)(2,1)} %bitcast.25, f32[64]{0:T(128)S(1)} %get-tuple-element.11, s32[64]{0:T(128)S(1)} %get-tuple-element.14, f32[64]{0:T(128)S(1)} %get-tuple-element.12, s32[64]{0:T(128)S(1)} %get-tuple-element.15, f32[64]{0:T(128)S(1)} %get-tuple-element.6, ...), kind=kOutput, calls=%fused_computation.8 | convolution fusion | flops 403472384 | bytes 1183744 | tf_op jit(solution)/shard_map/dot_general | solution.py:50
  (7 shorter events, 0.1 us)
Async XLA Ops:
  6.5 113.2 %copy-start = (bf16[1,384,4096]{2,1,0:T(8,128)(2,1)S(1)}, bf16[1,384,4096]{2,1,0:T(8,128)(2,1)}, u32[]{:S(2)}) copy-start(bf16[1,384,4096]{2,1,0:T(8,128)(2,1)} %param.11) | copy-start | bytes 9437188
  6.5 105.7 %all-gather.2.cloned.1.call-start = ((), (), s32[]{:S(2)}) async-start(), calls=%async_computation.3 | async-start | bytes 5242880 | tf_op jit(solution)/shard_map/all_gather | solution.py:33
  32.0 167.5 %reduce-scatter.2.cloned.1.call-start = ((), (), s32[]{:S(2)}) async-start(), calls=%async_computation.4 | async-start | bytes 5242880 | tf_op jit(solution)/shard_map/reduce_scatter | solution.py:41
  124.1 79.7 %copy-start.1 = (f32[64,8]{0,1:T(8,128)S(1)}, f32[64,8]{0,1:T(8,128)}, u32[]{:S(2)}) copy-start(f32[64,8]{0,1:T(8,128)} %param.8) | copy-start | bytes 6148
  199.5 19.6 %all-to-all-start.1 = ((bf16[1024,8,64]{0,2,1:T(8,128)(2,1)}), bf16[1024,8,64]{0,2,1:T(8,128)(2,1)}, u32[]{:S(2)}, u32[]{:S(2)}) async-start(bf16[1024,8,64]{0,2,1:T(8,128)(2,1)} %bitcast.56), calls=%async_computation.2 | async-start | bytes 2097152 | tf_op jit(solution)/shard_map/all_to_all | solution.py:49
Sparse Core Ops, SparseCore 0:
  32.1 80.0 all-gather.1
  124.2 75.2 reduce-scatter.1
where the time goes:
time: 229 us
  waiting for transfers between devices  171 us (75%)
  blocking collectives  20.4 us (9%)
  matrix products  16 us (7%)
  between operations  13.5 us (6%)
  starting transfers between devices  4.27 us (2%)
    all_gather x1, waiting for transfers between devices, local(): lax.all_gather(arrived, 'tensor', axis=1, tiled=True)  80.2 us
    reduce_scatter x1, waiting for transfers between devices, local(): lax.psum_scatter(lax.dot_general(down_rows, hidden, (((0,), (1,)), ((), (...  75.4 us
    all_to_all x1, blocking collectives, local(): lax.all_to_all(outgoing, 'expert', split_axis=0, concat_axis=0, tiled=True)  20.4 us
    all_to_all x1, waiting for transfers between devices, local(): lax.all_to_all(summed, 'expert', split_axis=1, concat_axis=1, tiled=True)  15.4 us
    dot_general x1, matrix products, local(): jnp.dot(lax.all_gather(arrived, 'tensor', axis=1, tiled=True), paired, pr...  7.47 us
  transfers between devices with their start and end apart: 3, of which 3 were waited for; matrix products, arithmetic and copies ran while one was open for 0% of the time, Pallas kernels for 0%

commit v1 on v0

--- a/solution.py
+++ b/solution.py
@@ -4,7 +4,7 @@
 from jax.sharding import PartitionSpec as P
 
 
-def local(tokens, expert_ids, gate_weights, w_gate, w_up, w_down):
+def slot_plan(tokens, expert_ids, gate_weights, w_gate, w_up, w_down):
     experts = lax.axis_size("expert")
     tok_rows, top_count = expert_ids.shape
     capacity = min(tok_rows, 3 * tok_rows * top_count // (2 * experts))
@@ -37,10 +37,9 @@
     hidden = (jax.nn.silu(gate_up[:, :hidden_units]) * gate_up[:, hidden_units:]).astype(
         jnp.bfloat16
     )
-    down_rows = w_down[0]
     summed = lax.psum_scatter(
         lax.dot_general(
-            down_rows, hidden, (((0,), (1,)), ((), ())), preferred_element_type=jnp.float32
+            w_down[0], hidden, (((0,), (1,)), ((), ())), preferred_element_type=jnp.float32
         ).astype(jnp.bfloat16),
         "tensor",
         scatter_dimension=0,
@@ -57,6 +56,114 @@
     return mixed.astype(jnp.bfloat16)
 
 
+def toward(a, axis, flip):
+    return lax.ppermute(a, axis, [(i, i ^ flip) for i in range(lax.axis_size(axis))])
+
+
+def f32(a):
+    return a.astype(jnp.float32)
+
+
+def half(a):
+    return a.astype(jnp.bfloat16)
+
+
+def spread(a):
+    mid = a.shape[0] // 2
+    ax = toward(a, "expert", 2)
+    ay = toward(a, "expert", 4)
+    far_a = toward(ax[:mid], "expert", 4)
+    far_b = toward(ay[mid:], "expert", 2)
+    mine = jnp.concatenate([a, ax, ay, far_a, far_b], axis=0)
+    other = toward(mine, "expert", 1)
+    return mine, other
+
+
+def collect(mine_of, other_of):
+    got = toward(half(other_of()), "expert", 1)
+    part = half(mine_of() + f32(got))
+    rows = part.shape[0] // 4
+    mid = rows // 2
+    own, px, py, pd = (part[i * rows : (i + 1) * rows] for i in range(4))
+    fx = toward(jnp.concatenate([px[:mid], pd[:mid]], axis=0), "expert", 2)
+    fy = toward(jnp.concatenate([py[mid:], pd[mid:]], axis=0), "expert", 4)
+    up = half(f32(py[:mid]) + f32(fx[mid:]))
+    down = half(f32(px[mid:]) + f32(fy[mid:]))
+    gy = toward(up, "expert", 4)
+    gx = toward(down, "expert", 2)
+    first = f32(own[:mid]) + f32(fx[:mid]) + f32(gy)
+    second = f32(own[mid:]) + f32(fy[:mid]) + f32(gx)
+    return jnp.concatenate([first, second], axis=0)
+
+
+def gather_plan(tokens, expert_ids, gate_weights, w_gate, w_up, w_down):
+    experts, shards = lax.axis_size("expert"), lax.axis_size("tensor")
+    me, mz = lax.axis_index("expert"), lax.axis_index("tensor")
+    _, cols = tokens.shape
+    units = w_gate.shape[2]
+    hits = expert_ids[:, :, None] == jnp.arange(experts, dtype=jnp.int32)
+    table = jnp.sum(jnp.where(hits, gate_weights[:, :, None], 0.0), axis=1)
+    terms, rest = [], table
+    for _ in range(3):
+        term = lax.reduce_precision(rest, 8, 7)
+        terms.append(half(term))
+        rest = rest - term
+    terms = jnp.concatenate(terms, axis=1)
+    terms = jnp.pad(terms, ((0, 0), (0, 128 - terms.shape[1])))
+
+    zs = {k: toward(tokens, "tensor", k) for k in range(1, shards)}
+    chunks = [[0], list(range(1, shards - 1)), [shards - 1]]
+    acc = [0.0, 0.0]
+    weight = None
+    for n, ks in enumerate(chunks):
+        parts = [tokens if k == 0 else zs[k] for k in ks]
+        if n == 1:
+            parts.append(terms)
+        both = spread(jnp.concatenate(parts, axis=1) if len(parts) > 1 else parts[0])
+        for i, k in enumerate(ks):
+            at = (mz ^ k) * cols
+            wk = jnp.concatenate(
+                [lax.dynamic_slice_in_dim(w[0], at, cols, 0) for w in (w_gate, w_up)], axis=1
+            )
+            for h in range(2):
+                acc[h] = acc[h] + jnp.dot(
+                    both[h][:, i * cols : (i + 1) * cols], wk, preferred_element_type=jnp.float32
+                )
+        if n == 1:
+            pick = jnp.arange(3 * experts, dtype=jnp.int32) % experts == me
+            weight = [
+                jnp.sum(jnp.where(pick, f32(b[:, len(ks) * cols :][:, : 3 * experts]), 0.0), axis=1)
+                for b in both
+            ]
+    hidden = [
+        half(jax.nn.silu(a[:, :units]) * a[:, units:] * w[:, None]) for a, w in zip(acc, weight)
+    ]
+    sums = {}
+    for n, ks in reversed(list(enumerate(chunks))):
+        wd = jnp.concatenate(
+            [lax.dynamic_slice_in_dim(w_down[0], (mz ^ k) * cols, cols, 1) for k in ks], axis=1
+        )
+        total = collect(
+            lambda: jnp.dot(hidden[0], wd, preferred_element_type=jnp.float32),
+            lambda: jnp.dot(hidden[1], wd, preferred_element_type=jnp.float32),
+        )
+        for i, k in enumerate(ks):
+            sums[k] = total[:, i * cols : (i + 1) * cols]
+    mixed = sums[0]
+    for k in range(1, shards):
+        mixed = mixed + f32(toward(half(sums[k]), "tensor", k))
+    return half(mixed)
+
+
+def local(*args):
+    tok_rows, top_count = args[1].shape
+    experts, shards = lax.axis_size("expert"), lax.axis_size("tensor")
+    capacity = min(tok_rows, 3 * tok_rows * top_count // (2 * experts))
+    if capacity == tok_rows and experts == 1 << 3 and shards & (shards - 1) == 0 and shards > 2:
+        return gather_plan(*args)
+    return slot_plan(*args)
+
+
 def solution(mesh):
     placed = (
         P("expert", "tensor"),

time: 229 us -> 98.3 us (0.43)
  waiting for transfers between devices: 171 us -> 30.2 us
  starting transfers between devices: 4.27 us -> 42.8 us
  blocking collectives: 20.4 us -> 0 us
  between operations: 13.5 us -> 0.54 us
  local copies, waits for them, and re-layouts: 1.49 us -> 12.1 us
  matrix products: 16 us -> 7.87 us
  other arithmetic: 1.98 us -> 4.36 us
    all_gather x1 -> x0, waiting for transfers between devices: 80.2 us -> none  [local(): lax.all_gather(arrived, 'tensor', axis=1, tiled=True)]
    reduce_scatter x1 -> x0, waiting for transfers between devices: 75.4 us -> none  [local(): lax.psum_scatter(lax.dot_general(down_rows, hidden, (((0,), (1,)), ((), (...]
    ppermute x0 -> x36, starting transfers between devices: none -> 42.8 us  [toward(): lax.ppermute(a, axis, [(i, i ^ flip) for i in range(lax.axis_size(axis))])]
    ppermute x0 -> x36, waiting for transfers between devices: none -> 30.2 us  [toward(): lax.ppermute(a, axis, [(i, i ^ flip) for i in range(lax.axis_size(axis))])]
    all_to_all x1 -> x0, blocking collectives: 20.4 us -> none  [local(): lax.all_to_all(outgoing, 'expert', split_axis=0, concat_axis=0, tiled=True)]
    all_to_all x1 -> x0, waiting for transfers between devices: 15.4 us -> none  [local(): lax.all_to_all(summed, 'expert', split_axis=1, concat_axis=1, tiled=True)]
    dot_general x4 -> x14, matrix products: 16 us -> 7.87 us  [the longest x8 4.67 us: gather_plan(): jnp.dot(both[h][:, i * cols:(i + 1) * cols], wk, preferred_element_type=j...]
    dynamic_slice x0 -> x2, local copies, waits for them, and re-layouts: none -> 5.8 us  [the longest x1 4.15 us: gather_plan(): lax.dynamic_slice_in_dim(w[0], at, cols, 0)]
  transfers between devices with their start and end apart: 3 -> 36, of which waited for: 3 -> 13; matrix products, arithmetic and copies ran while one was open for 0% -> 19% of each run, Pallas kernels for 0% -> 0%
where the time goes in v1:
time: 98.3 us; the launch traced here: 97.9 us
  starting transfers between devices  42.8 us (44%)
  waiting for transfers between devices  30.2 us (31%)
  local copies, waits for them, and re-layouts  12.1 us (12%)
  matrix products  7.87 us (8%)
  other arithmetic  4.36 us (4%)
    ppermute x36, starting transfers between devices, toward(): lax.ppermute(a, axis, [(i, i ^ flip) for i in range(lax.axis_size(axis))])  42.8 us
    ppermute x36, waiting for transfers between devices, toward(): lax.ppermute(a, axis, [(i, i ^ flip) for i in range(lax.axis_size(axis))])  30.2 us
    unnamed x30, local copies, waits for them, and re-layouts  6.18 us
    dot_general x8, matrix products, gather_plan(): jnp.dot(both[h][:, i * cols:(i + 1) * cols], wk, preferred_element_type=j...  4.67 us
    dynamic_slice x1, local copies, waits for them, and re-layouts, gather_plan(): lax.dynamic_slice_in_dim(w[0], at, cols, 0)  4.15 us
  transfers between devices with their start and end apart: 36, of which 13 were waited for; matrix products, arithmetic and copies ran while one was open for 19% of the time, Pallas kernels for 0%

profile of v1, /device:TPU:0, one launch (start us, length us, event | category | flops | bytes accessed | tf_op | source)
XLA Modules:
  0.0 97.9 jit_solution(12228455297306129470)
XLA Ops:
  0.0 3.1 %collective-permute-start.4 = (bf16[64,1024]{1,0:T(8,128)(2,1)}, bf16[64,1024]{1,0:T(8,128)(2,1)S(1)}, u32[]{:S(2)}, u32[]{:S(2)}) collective-permute-start(bf16[64,1024]{1,0:T(8,128)(2,1)} %param.6), channel_id=1, source_target_pairs={{0,1},{1,0},{2,3},{3,2},{4,5},{5,4},{6,7},{7,6},{8,9},{9,8},{10,11... | collective-permute-start | bytes 393224 | tf_op jit(solution)/shard_map/ppermute | solution.py:60
  3.1 2.6 %collective-permute-start.5 = (bf16[64,1024]{1,0:T(8,128)(2,1)}, bf16[64,1024]{1,0:T(8,128)(2,1)}, u32[]{:S(2)}, u32[]{:S(2)}) collective-permute-start(bf16[64,1024]{1,0:T(8,128)(2,1)} %param.6), channel_id=1, source_target_pairs={{0,2},{1,3},{2,0},{3,1},{4,6},{5,7},{6,4},{7,5},{8,10},{9,11},{10,... | collective-permute-start | bytes 393224 | tf_op jit(solution)/shard_map/ppermute | solution.py:60
  5.6 1.7 %collective-permute-start = (bf16[64,1024]{1,0:T(8,128)(2,1)}, bf16[64,1024]{1,0:T(8,128)(2,1)S(1)}, u32[]{:S(2)}, u32[]{:S(2)}) collective-permute-start(bf16[64,1024]{1,0:T(8,128)(2,1)} %param.6), channel_id=1, source_target_pairs={{0,8},{4,12},{8,0},{12,4},{16,24},{20,28},{24,16},{28,20},{1,9},{5... | collective-permute-start | bytes 393224 | tf_op jit(solution)/shard_map/ppermute | solution.py:60
  10.2 1.6 %dynamic-slice_bitcast_fusion.1 = (bf16[384,1024]{1,0:T(8,128)(2,1)S(1)}, bf16[384,1024]{1,0:T(8,128)(2,1)S(1)}) fusion(bf16[1,384,4096]{2,1,0:T(8,128)(2,1)} %param.11, s32[]{:T(128)S(6)} %select_n.40, s32[]{:T(128)S(6)} %select_n.41), kind=kLoop, calls=%fused_computation.31 | loop fusion | bytes 3145736 | tf_op jit(solution)/shard_map/dynamic_slice | solution.py:144
  12.6 4.2 %dynamic-slice_bitcast_fusion.8 = (bf16[1024,384]{1,0:T(8,128)(2,1)S(1)}, bf16[1024,384]{1,0:T(8,128)(2,1)}, bf16[1024,384]{1,0:T(8,128)(2,1)}, bf16[1024,384]{1...) fusion(bf16[1,4096,384]{2,1,0:T(8,128)(2,1)S(1)} %copy-done.1, ...), kind=kLoop, calls=%fused_computation.38 | loop fusion | bytes 12582928 | tf_op jit(solution)/shard_map/dynamic_slice | solution.py:126
  20.8 1.8 %collective-permute-start.2 = (bf16[32,1024]{1,0:T(8,128)(2,1)S(1)}, bf16[32,1024]{1,0:T(8,128)(2,1)S(1)}, u32[]{:S(2)}, u32[]{:S(2)}) collective-permute-start(bf16[32,1024]{1,0:T(8,128)(2,1)S(1)} %slice.258), channel_id=1, source_target_pairs={{0,16},{4,20},{8,24},{12,28},{16,0},{20,4},{24,8},{28,12},{1,17},{... | collective-permute-start | bytes 196616 | tf_op jit(solution)/shard_map/ppermute | solution.py:60
  22.7 1.6 %collective-permute-start.3 = (bf16[32,1024]{1,0:T(8,128)(2,1)S(1)}, bf16[32,1024]{1,0:T(8,128)(2,1)S(1)}, u32[]{:S(2)}, u32[]{:S(2)}) collective-permute-start(bf16[32,1024]{1,0:T(8,128)(2,1)S(1)} %slice.259), channel_id=1, source_target_pairs={{0,8},{4,12},{8,0},{12,4},{16,24},{20,28},{24,16},{28,20},{1,9},{5... | collective-permute-start | bytes 196616 | tf_op jit(solution)/shard_map/ppermute | solution.py:60
  25.7 3.0 %collective-permute-done.2 = bf16[32,1024]{1,0:T(8,128)(2,1)S(1)} collective-permute-done((bf16[32,1024]{1,0:T(8,128)(2,1)S(1)}, bf16[32,1024]{1,0:T(8,128)(2,1)S(1)}, u32[]{:S(2)}, u32[]{:S(2)}) %collective-permute-start.2) | collective-permute-done | bytes 65568 | tf_op jit(solution)/shard_map/ppermute | solution.py:60
  31.9 2.7 %collective-permute-done.12 = bf16[64,1024]{1,0:T(8,128)(2,1)S(1)} collective-permute-done((bf16[64,1024]{1,0:T(8,128)(2,1)}, bf16[64,1024]{1,0:T(8,128)(2,1)S(1)}, u32[]{:S(2)}, u32[]{:S(2)}) %collective-permute-start.12) | collective-permute-done | bytes 131104 | tf_op jit(solution)/shard_map/ppermute | solution.py:60
  36.2 2.7 %collective-permute-done.14 = bf16[32,1024]{1,0:T(8,128)(2,1)S(1)} collective-permute-done((bf16[32,1024]{1,0:T(8,128)(2,1)S(1)}, bf16[32,1024]{1,0:T(8,128)(2,1)S(1)}, u32[]{:S(2)}, u32[]{:S(2)}) %collective-permute-start.14) | collective-permute-done | bytes 65568 | tf_op jit(solution)/shard_map/ppermute | solution.py:60
  39.2 1.6 %collective-permute-start.9 = (bf16[32,2176]{1,0:T(8,128)(2,1)S(1)}, bf16[32,2176]{1,0:T(8,128)(2,1)S(1)}, u32[]{:S(2)}, u32[]{:S(2)}) collective-permute-start(bf16[32,2176]{1,0:T(8,128)(2,1)S(1)} %slice.261), channel_id=1, source_target_pairs={{0,8},{4,12},{8,0},{12,4},{16,24},{20,28},{24,16},{28,20},{1,9},{5... | collective-permute-start | bytes 417800 | tf_op jit(solution)/shard_map/ppermute | solution.py:60
  40.8 4.3 %collective-permute-done.8 = bf16[32,2176]{1,0:T(8,128)(2,1)S(1)} collective-permute-done((bf16[32,2176]{1,0:T(8,128)(2,1)S(1)}, bf16[32,2176]{1,0:T(8,128)(2,1)S(1)}, u32[]{:S(2)}, u32[]{:S(2)}) %collective-permute-start.8) | collective-permute-done | bytes 139296 | tf_op jit(solution)/shard_map/ppermute | solution.py:60
  56.5 1.8 %collective-permute-start.33 = (bf16[64,1024]{1,0:T(8,128)(2,1)S(1)}, bf16[64,1024]{1,0:T(8,128)(2,1)S(1)}, u32[]{:S(2)}, u32[]{:S(2)}) collective-permute-start(bf16[64,1024]{1,0:T(8,128)(2,1)S(1)} %pad_maximum_fusion.22), channel_id=1, source_target_pairs={{0,16},{4,20},{8,24},{12,28},{16,0},{20,4},{24,8},{28,12},{1,17},{... | collective-permute-start | bytes 393224 | tf_op jit(solution)/shard_map/ppermute | solution.py:60
  58.3 1.6 %collective-permute-start.31 = (bf16[64,1024]{1,0:T(8,128)(2,1)S(1)}, bf16[64,1024]{1,0:T(8,128)(2,1)S(1)}, u32[]{:S(2)}, u32[]{:S(2)}) collective-permute-start(bf16[64,1024]{1,0:T(8,128)(2,1)S(1)} %pad_maximum_fusion.21), channel_id=1, source_target_pairs={{0,8},{4,12},{8,0},{12,4},{16,24},{20,28},{24,16},{28,20},{1,9},{5... | collective-permute-start | bytes 393224 | tf_op jit(solution)/shard_map/ppermute | solution.py:60
  63.7 1.8 %collective-permute-start.32 = (bf16[32,1024]{1,0:T(8,128)(2,1)S(1)}, bf16[32,1024]{1,0:T(8,128)(2,1)S(1)}, u32[]{:S(2)}, u32[]{:S(2)}) collective-permute-start(bf16[32,1024]{1,0:T(8,128)(2,1)S(1)} %add_convert_fusion.8), channel_id=1, source_target_pairs={{0,16},{4,20},{8,24},{12,28},{16,0},{20,4},{24,8},{28,12},{1,17},{... | collective-permute-start | bytes 196616 | tf_op jit(solution)/shard_map/ppermute | solution.py:60
  65.5 5.3 %collective-permute-done.24 = bf16[64,2048]{1,0:T(8,128)(2,1)S(1)} collective-permute-done((bf16[64,2048]{1,0:T(8,128)(2,1)S(1)}, bf16[64,2048]{1,0:T(8,128)(2,1)S(1)}, u32[]{:S(2)}, u32[]{:S(2)}) %collective-permute-start.24) | collective-permute-done | bytes 262176 | tf_op jit(solution)/shard_map/ppermute | solution.py:60
  73.6 3.0 %collective-permute-done.25 = bf16[32,2048]{1,0:T(8,128)(2,1)S(1)} collective-permute-done((bf16[32,2048]{1,0:T(8,128)(2,1)S(1)}, bf16[32,2048]{1,0:T(8,128)(2,1)S(1)}, u32[]{:S(2)}, u32[]{:S(2)}) %collective-permute-start.25) | collective-permute-done | bytes 131104 | tf_op jit(solution)/shard_map/ppermute | solution.py:60
  76.7 1.9 %collective-permute-start.26 = (bf16[64,2048]{1,0:T(8,128)(2,1)S(1)}, bf16[64,2048]{1,0:T(8,128)(2,1)S(1)}, u32[]{:S(2)}, u32[]{:S(2)}) collective-permute-start(bf16[64,2048]{1,0:T(8,128)(2,1)S(1)} %pad_maximum_fusion.18), channel_id=1, source_target_pairs={{0,16},{4,20},{8,24},{12,28},{16,0},{20,4},{24,8},{28,12},{1,17},{... | collective-permute-start | bytes 786440 | tf_op jit(solution)/shard_map/ppermute | solution.py:60
  78.8 2.0 %collective-permute-start.22 = (bf16[32,1024]{1,0:T(8,128)(2,1)S(1)}, bf16[32,1024]{1,0:T(8,128)(2,1)S(1)}, u32[]{:S(2)}, u32[]{:S(2)}) collective-permute-start(bf16[32,1024]{1,0:T(8,128)(2,1)S(1)} %get-tuple-element.29), channel_id=1, source_target_pairs={{0,8},{4,12},{8,0},{12,4},{16,24},{20,28},{24,16},{28,20},{1,9},{5... | collective-permute-start | bytes 196616 | tf_op jit(solution)/shard_map/ppermute | solution.py:60
  80.8 2.3 %collective-permute-done.26 = bf16[64,2048]{1,0:T(8,128)(2,1)S(1)} collective-permute-done((bf16[64,2048]{1,0:T(8,128)(2,1)S(1)}, bf16[64,2048]{1,0:T(8,128)(2,1)S(1)}, u32[]{:S(2)}, u32[]{:S(2)}) %collective-permute-start.26) | collective-permute-done | bytes 262176 | tf_op jit(solution)/shard_map/ppermute | solution.py:60
  83.1 1.9 %collective-permute-start.27 = (bf16[32,2048]{1,0:T(8,128)(2,1)S(1)}, bf16[32,2048]{1,0:T(8,128)(2,1)S(1)}, u32[]{:S(2)}, u32[]{:S(2)}) collective-permute-start(bf16[32,2048]{1,0:T(8,128)(2,1)S(1)} %add_convert_fusion.3), channel_id=1, source_target_pairs={{0,8},{4,12},{8,0},{12,4},{16,24},{20,28},{24,16},{28,20},{1,9},{5... | collective-permute-start | bytes 393224 | tf_op jit(solution)/shard_map/ppermute | solution.py:60
  85.1 3.6 %collective-permute-start.35 = (bf16[64,1024]{1,0:T(8,128)(2,1)S(1)}, bf16[64,1024]{1,0:T(8,128)(2,1)S(1)}, u32[]{:S(2)}, u32[]{:S(2)}) collective-permute-start(bf16[64,1024]{1,0:T(8,128)(2,1)S(1)} %pad_maximum_fusion.23), channel_id=1, source_target_pairs={{0,3},{1,2},{2,1},{3,0},{4,7},{5,6},{6,5},{7,4},{8,11},{9,10},{10,... | collective-permute-start | bytes 393224 | tf_op jit(solution)/shard_map/ppermute | solution.py:60
  88.9 3.5 %collective-permute-start.29 = (bf16[64,1024]{1,0:T(8,128)(2,1)S(1)}, bf16[64,1024]{1,0:T(8,128)(2,1)S(1)}, u32[]{:S(2)}, u32[]{:S(2)}) collective-permute-start(bf16[64,1024]{1,0:T(8,128)(2,1)S(1)} %get-tuple-element.37), channel_id=1, source_target_pairs={{0,2},{1,3},{2,0},{3,1},{4,6},{5,7},{6,4},{7,5},{8,10},{9,11},{10,... | collective-permute-start | bytes 393224 | tf_op jit(solution)/shard_map/ppermute | solution.py:60
  93.4 2.3 %collective-permute-done.28 = bf16[64,1024]{1,0:T(8,128)(2,1)S(1)} collective-permute-done((bf16[64,1024]{1,0:T(8,128)(2,1)S(1)}, bf16[64,1024]{1,0:T(8,128)(2,1)S(1)}, u32[]{:S(2)}, u32[]{:S(2)}) %collective-permute-start.28) | collective-permute-done | bytes 131104 | tf_op jit(solution)/shard_map/ppermute | solution.py:60
  (134 shorter events, 35.8 us)
Async XLA Ops:
  0.0 19.0 %collective-permute-start.4 = (bf16[64,1024]{1,0:T(8,128)(2,1)}, bf16[64,1024]{1,0:T(8,128)(2,1)S(1)}, u32[]{:S(2)}, u32[]{:S(2)}) collective-permute-start(bf16[64,1024]{1,0:T(8,128)(2,1)} %param.6), channel_id=1, source_target_pairs={{0,1},{1,0},{2,3},{3,2},{4,5},{5,4},{6,7},{7,6},{8,9},{9,8},{10,11... | collective-permute-start | bytes 393224 | tf_op jit(solution)/shard_map/ppermute | solution.py:60
  3.1 15.9 %collective-permute-start.5 = (bf16[64,1024]{1,0:T(8,128)(2,1)}, bf16[64,1024]{1,0:T(8,128)(2,1)}, u32[]{:S(2)}, u32[]{:S(2)}) collective-permute-start(bf16[64,1024]{1,0:T(8,128)(2,1)} %param.6), channel_id=1, source_target_pairs={{0,2},{1,3},{2,0},{3,1},{4,6},{5,7},{6,4},{7,5},{8,10},{9,11},{10,... | collective-permute-start | bytes 393224 | tf_op jit(solution)/shard_map/ppermute | solution.py:60
  5.6 18.6 %collective-permute-start.10 = (bf16[64,1024]{1,0:T(8,128)(2,1)}, bf16[64,1024]{1,0:T(8,128)(2,1)}, u32[]{:S(2)}, u32[]{:S(2)}) collective-permute-start(bf16[64,1024]{1,0:T(8,128)(2,1)} %param.6), channel_id=1, source_target_pairs={{0,3},{1,2},{2,1},{3,0},{4,7},{5,6},{6,5},{7,4},{8,11},{9,10},{10,... | collective-permute-start | bytes 393224 | tf_op jit(solution)/shard_map/ppermute | solution.py:60
  5.6 15.2 %collective-permute-start = (bf16[64,1024]{1,0:T(8,128)(2,1)}, bf16[64,1024]{1,0:T(8,128)(2,1)S(1)}, u32[]{:S(2)}, u32[]{:S(2)}) collective-permute-start(bf16[64,1024]{1,0:T(8,128)(2,1)} %param.6), channel_id=1, source_target_pairs={{0,8},{4,12},{8,0},{12,4},{16,24},{20,28},{24,16},{28,20},{1,9},{5... | collective-permute-start | bytes 393224 | tf_op jit(solution)/shard_map/ppermute | solution.py:60
  7.4 15.3 %collective-permute-start.1 = (bf16[64,1024]{1,0:T(8,128)(2,1)}, bf16[64,1024]{1,0:T(8,128)(2,1)S(1)}, u32[]{:S(2)}, u32[]{:S(2)}) collective-permute-start(bf16[64,1024]{1,0:T(8,128)(2,1)} %param.6), channel_id=1, source_target_pairs={{0,16},{4,20},{8,24},{12,28},{16,0},{20,4},{24,8},{28,12},{1,17},{... | collective-permute-start | bytes 393224 | tf_op jit(solution)/shard_map/ppermute | solution.py:60
  19.9 19.0 %collective-permute-start.6 = (bf16[64,2176]{1,0:T(8,128)(2,1)S(1)}, bf16[64,2176]{1,0:T(8,128)(2,1)S(1)}, u32[]{:S(2)}, u32[]{:S(2)}) collective-permute-start(bf16[64,2176]{1,0:T(8,128)(2,1)S(1)} %get-tuple-element.34), channel_id=1, source_target_pairs={{0,8},{4,12},{8,0},{12,4},{16,24},{20,28},{24,16},{28,20},{1,9},{5... | collective-permute-start | bytes 835592 | tf_op jit(solution)/shard_map/ppermute | solution.py:60
  20.5 18.6 %collective-permute-start.7 = (bf16[64,2176]{1,0:T(8,128)(2,1)S(1)}, bf16[64,2176]{1,0:T(8,128)(2,1)S(1)}, u32[]{:S(2)}, u32[]{:S(2)}) collective-permute-start(bf16[64,2176]{1,0:T(8,128)(2,1)S(1)} %get-tuple-element.34), channel_id=1, source_target_pairs={{0,16},{4,20},{8,24},{12,28},{16,0},{20,4},{24,8},{28,12},{1,17},{... | collective-permute-start | bytes 835592 | tf_op jit(solution)/shard_map/ppermute | solution.py:60
  20.8 7.9 %collective-permute-start.2 = (bf16[32,1024]{1,0:T(8,128)(2,1)S(1)}, bf16[32,1024]{1,0:T(8,128)(2,1)S(1)}, u32[]{:S(2)}, u32[]{:S(2)}) collective-permute-start(bf16[32,1024]{1,0:T(8,128)(2,1)S(1)} %slice.258), channel_id=1, source_target_pairs={{0,16},{4,20},{8,24},{12,28},{16,0},{20,4},{24,8},{28,12},{1,17},{... | collective-permute-start | bytes 196616 | tf_op jit(solution)/shard_map/ppermute | solution.py:60
  22.7 7.2 %collective-permute-start.3 = (bf16[32,1024]{1,0:T(8,128)(2,1)S(1)}, bf16[32,1024]{1,0:T(8,128)(2,1)S(1)}, u32[]{:S(2)}, u32[]{:S(2)}) collective-permute-start(bf16[32,1024]{1,0:T(8,128)(2,1)S(1)} %slice.259), channel_id=1, source_target_pairs={{0,8},{4,12},{8,0},{12,4},{16,24},{20,28},{24,16},{28,20},{1,9},{5... | collective-permute-start | bytes 196616 | tf_op jit(solution)/shard_map/ppermute | solution.py:60
  24.2 7.1 %collective-permute-start.11 = (bf16[64,1024]{1,0:T(8,128)(2,1)}, bf16[64,1024]{1,0:T(8,128)(2,1)S(1)}, u32[]{:S(2)}, u32[]{:S(2)}) collective-permute-start(bf16[64,1024]{1,0:T(8,128)(2,1)} %collective-permute-done.10), channel_id=1, source_target_pairs={{0,8},{4,12},{8,0},{12,4},{16,24},{20,28},{24,16},{28,20},{1,9},{5... | collective-permute-start | bytes 393224 | tf_op jit(solution)/shard_map/ppermute | solution.py:60
  29.9 21.3 %collective-permute-start.15 = (bf16[256,1024]{1,0:T(8,128)(2,1)S(1)}, bf16[256,1024]{1,0:T(8,128)(2,1)S(1)}, u32[]{:S(2)}, u32[]{:S(2)}) collective-permute-start(bf16[256,1024]{1,0:T(8,128)(2,1)S(1)} %constant_dynamic-update-slice_fusion), channel_id=1, source_target_pairs={{0,4},{4,0},{8,12},{12,8},{16,20},{20,16},{24,28},{28,24},{1,5},{5... | collective-permute-start | bytes 1572872 | tf_op jit(solution)/shard_map/ppermute | solution.py:60
  38.9 10.4 %collective-permute-start.17 = (bf16[256,1024]{1,0:T(8,128)(2,1)S(1)}, bf16[256,1024]{1,0:T(8,128)(2,1)S(1)}, u32[]{:S(2)}, u32[]{:S(2)}) collective-permute-start(bf16[256,1024]{1,0:T(8,128)(2,1)S(1)} %constant_dynamic-update-slice_fusion.10), channel_id=1, source_target_pairs={{0,4},{4,0},{8,12},{12,8},{16,20},{20,16},{24,28},{28,24},{1,5},{5... | collective-permute-start | bytes 1572872 | tf_op jit(solution)/shard_map/ppermute | solution.py:60
  56.5 22.0 %collective-permute-start.33 = (bf16[64,1024]{1,0:T(8,128)(2,1)S(1)}, bf16[64,1024]{1,0:T(8,128)(2,1)S(1)}, u32[]{:S(2)}, u32[]{:S(2)}) collective-permute-start(bf16[64,1024]{1,0:T(8,128)(2,1)S(1)} %pad_maximum_fusion.22), channel_id=1, source_target_pairs={{0,16},{4,20},{8,24},{12,28},{16,0},{20,4},{24,8},{28,12},{1,17},{... | collective-permute-start | bytes 393224 | tf_op jit(solution)/shard_map/ppermute | solution.py:60
  60.3 18.4 %collective-permute-start.21 = (bf16[64,1024]{1,0:T(8,128)(2,1)S(1)}, bf16[64,1024]{1,0:T(8,128)(2,1)S(1)}, u32[]{:S(2)}, u32[]{:S(2)}) collective-permute-start(bf16[64,1024]{1,0:T(8,128)(2,1)S(1)} %pad_maximum_fusion.20), channel_id=1, source_target_pairs={{0,16},{4,20},{8,24},{12,28},{16,0},{20,4},{24,8},{28,12},{1,17},{... | collective-permute-start | bytes 393224 | tf_op jit(solution)/shard_map/ppermute | solution.py:60
  61.5 9.2 %collective-permute-start.24 = (bf16[64,2048]{1,0:T(8,128)(2,1)S(1)}, bf16[64,2048]{1,0:T(8,128)(2,1)S(1)}, u32[]{:S(2)}, u32[]{:S(2)}) collective-permute-start(bf16[64,2048]{1,0:T(8,128)(2,1)S(1)} %pad_maximum_fusion.17), channel_id=1, source_target_pairs={{0,8},{4,12},{8,0},{12,4},{16,24},{20,28},{24,16},{28,20},{1,9},{5... | collective-permute-start | bytes 786440 | tf_op jit(solution)/shard_map/ppermute | solution.py:60
  62.9 9.4 %collective-permute-start.19 = (bf16[64,1024]{1,0:T(8,128)(2,1)S(1)}, bf16[64,1024]{1,0:T(8,128)(2,1)S(1)}, u32[]{:S(2)}, u32[]{:S(2)}) collective-permute-start(bf16[64,1024]{1,0:T(8,128)(2,1)S(1)} %pad_maximum_fusion.19), channel_id=1, source_target_pairs={{0,8},{4,12},{8,0},{12,4},{16,24},{20,28},{24,16},{28,20},{1,9},{5... | collective-permute-start | bytes 393224 | tf_op jit(solution)/shard_map/ppermute | solution.py:60
  63.7 14.8 %collective-permute-start.32 = (bf16[32,1024]{1,0:T(8,128)(2,1)S(1)}, bf16[32,1024]{1,0:T(8,128)(2,1)S(1)}, u32[]{:S(2)}, u32[]{:S(2)}) collective-permute-start(bf16[32,1024]{1,0:T(8,128)(2,1)S(1)} %add_convert_fusion.8), channel_id=1, source_target_pairs={{0,16},{4,20},{8,24},{12,28},{16,0},{20,4},{24,8},{28,12},{1,17},{... | collective-permute-start | bytes 196616 | tf_op jit(solution)/shard_map/ppermute | solution.py:60
  72.3 6.5 %collective-permute-start.20 = (bf16[32,1024]{1,0:T(8,128)(2,1)S(1)}, bf16[32,1024]{1,0:T(8,128)(2,1)S(1)}, u32[]{:S(2)}, u32[]{:S(2)}) collective-permute-start(bf16[32,1024]{1,0:T(8,128)(2,1)S(1)} %add_convert_fusion.10), channel_id=1, source_target_pairs={{0,16},{4,20},{8,24},{12,28},{16,0},{20,4},{24,8},{28,12},{1,17},{... | collective-permute-start | bytes 196616 | tf_op jit(solution)/shard_map/ppermute | solution.py:60
  76.7 6.4 %collective-permute-start.26 = (bf16[64,2048]{1,0:T(8,128)(2,1)S(1)}, bf16[64,2048]{1,0:T(8,128)(2,1)S(1)}, u32[]{:S(2)}, u32[]{:S(2)}) collective-permute-start(bf16[64,2048]{1,0:T(8,128)(2,1)S(1)} %pad_maximum_fusion.18), channel_id=1, source_target_pairs={{0,16},{4,20},{8,24},{12,28},{16,0},{20,4},{24,8},{28,12},{1,17},{... | collective-permute-start | bytes 786440 | tf_op jit(solution)/shard_map/ppermute | solution.py:60
  78.6 6.5 %collective-permute-start.34 = (bf16[32,1024]{1,0:T(8,128)(2,1)S(1)}, bf16[32,1024]{1,0:T(8,128)(2,1)S(1)}, u32[]{:S(2)}, u32[]{:S(2)}) collective-permute-start(bf16[32,1024]{1,0:T(8,128)(2,1)S(1)} %get-tuple-element.23), channel_id=1, source_target_pairs={{0,8},{4,12},{8,0},{12,4},{16,24},{20,28},{24,16},{28,20},{1,9},{5... | collective-permute-start | bytes 196616 | tf_op jit(solution)/shard_map/ppermute | solution.py:60
  78.8 13.6 %collective-permute-start.22 = (bf16[32,1024]{1,0:T(8,128)(2,1)S(1)}, bf16[32,1024]{1,0:T(8,128)(2,1)S(1)}, u32[]{:S(2)}, u32[]{:S(2)}) collective-permute-start(bf16[32,1024]{1,0:T(8,128)(2,1)S(1)} %get-tuple-element.29), channel_id=1, source_target_pairs={{0,8},{4,12},{8,0},{12,4},{16,24},{20,28},{24,16},{28,20},{1,9},{5... | collective-permute-start | bytes 196616 | tf_op jit(solution)/shard_map/ppermute | solution.py:60
  85.1 8.3 %collective-permute-start.35 = (bf16[64,1024]{1,0:T(8,128)(2,1)S(1)}, bf16[64,1024]{1,0:T(8,128)(2,1)S(1)}, u32[]{:S(2)}, u32[]{:S(2)}) collective-permute-start(bf16[64,1024]{1,0:T(8,128)(2,1)S(1)} %pad_maximum_fusion.23), channel_id=1, source_target_pairs={{0,3},{1,2},{2,1},{3,0},{4,7},{5,6},{6,5},{7,4},{8,11},{9,10},{10,... | collective-permute-start | bytes 393224 | tf_op jit(solution)/shard_map/ppermute | solution.py:60
  88.9 6.8 %collective-permute-start.28 = (bf16[64,1024]{1,0:T(8,128)(2,1)S(1)}, bf16[64,1024]{1,0:T(8,128)(2,1)S(1)}, u32[]{:S(2)}, u32[]{:S(2)}) collective-permute-start(bf16[64,1024]{1,0:T(8,128)(2,1)S(1)} %get-tuple-element.36), channel_id=1, source_target_pairs={{0,1},{1,0},{2,3},{3,2},{4,5},{5,4},{6,7},{7,6},{8,9},{9,8},{10,11... | collective-permute-start | bytes 393224 | tf_op jit(solution)/shard_map/ppermute | solution.py:60
  88.9 8.3 %collective-permute-start.29 = (bf16[64,1024]{1,0:T(8,128)(2,1)S(1)}, bf16[64,1024]{1,0:T(8,128)(2,1)S(1)}, u32[]{:S(2)}, u32[]{:S(2)}) collective-permute-start(bf16[64,1024]{1,0:T(8,128)(2,1)S(1)} %get-tuple-element.37), channel_id=1, source_target_pairs={{0,2},{1,3},{2,0},{3,1},{4,6},{5,7},{6,4},{7,5},{8,10},{9,11},{10,... | collective-permute-start | bytes 393224 | tf_op jit(solution)/shard_map/ppermute | solution.py:60
  (21 other events, 99.5 us)

commit v2 on v1

--- a/solution.py
+++ b/solution.py
@@ -1,7 +1,14 @@
 import jax
 import jax.numpy as jnp
 from jax import lax
+from jax.experimental import pallas as pl
+from jax.experimental.pallas import tpu as pltpu
 from jax.sharding import PartitionSpec as P
+
+
+IN_CHUNKS = [[0], [1], [2], [3]]
+OUT_CHUNKS = [[3], [2], [1], [0]]
+TERMS_IN = 2
 
 
 def slot_plan(tokens, expert_ids, gate_weights, w_gate, w_up, w_down):
@@ -56,8 +63,30 @@
     return mixed.astype(jnp.bfloat16)
 
 
-def toward(a, axis, flip):
-    return lax.ppermute(a, axis, [(i, i ^ flip) for i in range(lax.axis_size(axis))])
+def toward(a, move):
+    experts, shards = lax.axis_size("expert"), lax.axis_size("tensor")
+    pairs = []
+    for e in range(experts):
+        for z in range(shards):
+            to_e, to_z = move(e, z)
+            pairs.append((e * shards + z, to_e * shards + to_z))
+    return lax.ppermute(a, ("expert", "tensor"), pairs)
+
+
+def core_pair(a):
+    return toward(a, lambda e, z: (e ^ 1, z))
+
+
+def first_side(a):
+    return toward(a, lambda e, z: (e ^ (2 << (e & 1)), z))
+
+
+def second_side(a):
+    return toward(a, lambda e, z: (e ^ (4 >> (e & 1)), z))
+
+
+def along(a, k):
+    return toward(a, lambda e, z: (e, z ^ k))
 
 
 def f32(a):
@@ -68,38 +97,63 @@
     return a.astype(jnp.bfloat16)
 
 
+def load_slices(places, sources, dim, grant):
+    shard = sources[0].shape[dim] // lax.axis_size("tensor")
+    shape = list(sources[0].shape[1:])
+    shape[dim - 1] = shard
+    width, count = shape[1], places.shape[0]
+
+    def kernel(places_ref, *refs):
+        ins, outs, sem = refs[: len(sources)], refs[len(sources) : -1], refs[-1]
+        copies = []
+        for k in range(count):
+            part = pl.ds(pl.multiple_of(places_ref[k] * shard, shard), shard)
+            for n, ref in enumerate(ins):
+                src = ref.at[0, part, :] if dim == 1 else ref.at[0, :, part]
+                dst = outs[k].at[:, pl.ds(n * width, width)]
+                copies.append(pltpu.make_async_copy(src, dst, sem.at[len(copies)]))
+        for copy in copies:
+            copy.start()
+        for copy in copies:
+            copy.wait()
+
+    out = pltpu.VMEM((shape[0], width * len(sources)), sources[0].dtype)
+    return pl.pallas_call(
+        kernel,
+        out_shape=[out] * count,
+        in_specs=[pl.BlockSpec(memory_space=pltpu.SMEM)]
+        + [pl.BlockSpec(memory_space=pl.ANY)] * len(sources),
+        out_specs=[pl.BlockSpec(memory_space=pltpu.VMEM)] * count,
+        scratch_shapes=[pltpu.SemaphoreType.DMA((count * len(sources),))],
+        compiler_params=pltpu.CompilerParams(vmem_limit_bytes=grant),
+    )(places, *[pltpu.with_memory_space_constraint(a, pltpu.HBM) for a in sources])
+
+
 def spread(a):
-    mid = a.shape[0] // 2
-    ax = toward(a, "expert", 2)
-    ay = toward(a, "expert", 4)
-    far_a = toward(ax[:mid], "expert", 4)
-    far_b = toward(ay[mid:], "expert", 2)
-    mine = jnp.concatenate([a, ax, ay, far_a, far_b], axis=0)
-    other = toward(mine, "expert", 1)
-    return mine, other
+    rows = a.shape[0]
+    pair = core_pair(a)
+    side = first_side(jnp.concatenate([a, pair], axis=0))
+    far = second_side(side[:rows])
+    brought = jnp.concatenate([side, far], axis=0)
+    swapped = core_pair(brought)
+    return jnp.concatenate([a, brought], axis=0), jnp.concatenate([pair, swapped], axis=0)
 
 
 def collect(mine_of, other_of):
-    got = toward(half(other_of()), "expert", 1)
+    got = core_pair(half(other_of()))
     part = half(mine_of() + f32(got))
     rows = part.shape[0] // 4
-    mid = rows // 2
-    own, px, py, pd = (part[i * rows : (i + 1) * rows] for i in range(4))
-    fx = toward(jnp.concatenate([px[:mid], pd[:mid]], axis=0), "expert", 2)
-    fy = toward(jnp.concatenate([py[mid:], pd[mid:]], axis=0), "expert", 4)
-    up = half(f32(py[:mid]) + f32(fx[mid:]))
-    down = half(f32(px[mid:]) + f32(fy[mid:]))
-    gy = toward(up, "expert", 4)
-    gx = toward(down, "expert", 2)
-    first = f32(own[:mid]) + f32(fx[:mid]) + f32(gy)
-    second = f32(own[mid:]) + f32(fy[:mid]) + f32(gx)
-    return jnp.concatenate([first, second], axis=0)
+    far = second_side(part[3 * rows :])
+    near = half(f32(part[rows : 2 * rows]) + f32(far))
+    side = first_side(jnp.concatenate([near, part[2 * rows : 3 * rows]], axis=0))
+    swapped = core_pair(side[rows:])
+    return f32(part[:rows]) + f32(side[:rows]) + f32(swapped)
 
 
 def gather_plan(tokens, expert_ids, gate_weights, w_gate, w_up, w_down):
     experts, shards = lax.axis_size("expert"), lax.axis_size("tensor")
     me, mz = lax.axis_index("expert"), lax.axis_index("tensor")
-    _, cols = tokens.shape
+    cols = tokens.shape[1]
     units = w_gate.shape[2]
     hits = expert_ids[:, :, None] == jnp.arange(experts, dtype=jnp.int32)
     table = jnp.sum(jnp.where(hits, gate_weights[:, :, None], 0.0), axis=1)
@@ -111,25 +165,26 @@
     terms = jnp.concatenate(terms, axis=1)
     terms = jnp.pad(terms, ((0, 0), (0, 128 - terms.shape[1])))
 
-    zs = {k: toward(tokens, "tensor", k) for k in range(1, shards)}
-    chunks = [[0], list(range(1, shards - 1)), [shards - 1]]
+    places = mz ^ jnp.arange(shards, dtype=jnp.int32)
+    pairs = load_slices(places, [w_gate, w_up], 1, 2 << 20)
+    downs = load_slices(places, [w_down], 2, 2 << 20)
+    zs = {k: along(tokens, k) for k in range(1, shards)}
     acc = [0.0, 0.0]
     weight = None
-    for n, ks in enumerate(chunks):
+    for n, ks in enumerate(IN_CHUNKS):
         parts = [tokens if k == 0 else zs[k] for k in ks]
-        if n == 1:
+        if n == TERMS_IN:
             parts.append(terms)
         both = spread(jnp.concatenate(parts, axis=1) if len(parts) > 1 else parts[0])
         for i, k in enumerate(ks):
-            at = (mz ^ k) * cols
-            wk = jnp.concatenate(
-                [lax.dynamic_slice_in_dim(w[0], at, cols, 0) for w in (w_gate, w_up)], axis=1
-            )
             for h in range(2):
                 acc[h] = acc[h] + jnp.dot(
-                    both[h][:, i * cols : (i + 1) * cols], wk, preferred_element_type=jnp.float32
+                    both[h][:, i * cols : (i + 1) * cols],
+                    pairs[k],
+                    preferred_element_type=jnp.float32,
                 )
-        if n == 1:
+        acc = list(lax.optimization_barrier(tuple(acc)))
+        if n == TERMS_IN:
             pick = jnp.arange(3 * experts, dtype=jnp.int32) % experts == me
             weight = [
                 jnp.sum(jnp.where(pick, f32(b[:, len(ks) * cols :][:, : 3 * experts]), 0.0), axis=1)
@@ -139,19 +194,21 @@
         half(jax.nn.silu(a[:, :units]) * a[:, units:] * w[:, None]) for a, w in zip(acc, weight)
     ]
     sums = {}
-    for n, ks in reversed(list(enumerate(chunks))):
-        wd = jnp.concatenate(
-            [lax.dynamic_slice_in_dim(w_down[0], (mz ^ k) * cols, cols, 1) for k in ks], axis=1
-        )
-        total = collect(
-            lambda: jnp.dot(hidden[0], wd, preferred_element_type=jnp.float32),
-            lambda: jnp.dot(hidden[1], wd, preferred_element_type=jnp.float32),
-        )
+    for ks in OUT_CHUNKS:
+        def product(h):
+            return jnp.concatenate(
+                [jnp.dot(hidden[h], downs[k], preferred_element_type=jnp.float32) for k in ks],
+                axis=1,
+            )
+
+        total = collect(lambda: product(0), lambda: product(1))
         for i, k in enumerate(ks):
             sums[k] = total[:, i * cols : (i + 1) * cols]
+            if k:
+                sums[k] = half(sums[k])
     mixed = sums[0]
     for k in range(1, shards):
-        mixed = mixed + f32(toward(half(sums[k]), "tensor", k))
+        mixed = mixed + f32(along(sums[k], k))
     return half(mixed)
 
 

time: 98.3 us -> 82.6 us (0.84)
  local copies, waits for them, and re-layouts: 12.1 us -> 0.33 us
  Pallas kernels: 0 us -> 5.84 us
  starting transfers between devices: 42.8 us -> 37.5 us
  waiting for transfers between devices: 30.2 us -> 27.6 us
  other arithmetic: 4.36 us -> 2.56 us
    unnamed x30 -> x4, local copies, waits for them, and re-layouts: 6.18 us -> 0.12 us
    pallas_call x0 -> x2, Pallas kernels: none -> 5.84 us  [load_slices(): pl.pallas_call(kernel, out_shape=[out] * count, in_specs=[pl.BlockSpec(me...]
    dynamic_slice x2 -> x0, local copies, waits for them, and re-layouts: 5.8 us -> none  [the longest x1 4.15 us: gather_plan(): lax.dynamic_slice_in_dim(w[0], at, cols, 0)]
    ppermute x36 -> x38, starting transfers between devices: 42.8 us -> 37.5 us  [toward(): return lax.ppermute(a, ('expert', 'tensor'), pairs)]
    ppermute x36 -> x38, waiting for transfers between devices: 30.2 us -> 27.6 us  [toward(): return lax.ppermute(a, ('expert', 'tensor'), pairs)]
    dot_general x14 -> x16, matrix products: 7.87 us -> 8.1 us  [the longest x8 4.58 us: gather_plan(): jnp.dot(both[h][:, i * cols:(i + 1) * cols], pairs[k], preferred_element_...]
  transfers between devices with their start and end apart: 36 -> 38, of which waited for: 13 -> 11; matrix products, arithmetic and copies ran while one was open for 19% -> 11% of each run, Pallas kernels for 0% -> 7%
where the time goes in v2:
time: 82.6 us; the launch traced here: 82.4 us
  starting transfers between devices  37.5 us (45%)
  waiting for transfers between devices  27.6 us (33%)
  matrix products  8.1 us (10%)
  Pallas kernels  5.84 us (7%)
  other arithmetic  2.56 us (3%)
    ppermute x38, starting transfers between devices, toward(): return lax.ppermute(a, ('expert', 'tensor'), pairs)  37.5 us
    ppermute x38, waiting for transfers between devices, toward(): return lax.ppermute(a, ('expert', 'tensor'), pairs)  27.6 us
    pallas_call x2, Pallas kernels, load_slices(): pl.pallas_call(kernel, out_shape=[out] * count, in_specs=[pl.BlockSpec(me...  5.84 us
    dot_general x8, matrix products, gather_plan(): jnp.dot(both[h][:, i * cols:(i + 1) * cols], pairs[k], preferred_element_...  4.58 us
    dot_general x8, matrix products, product(): jnp.dot(hidden[h], downs[k], preferred_element_type=jnp.float32)  3.52 us
  transfers between devices with their start and end apart: 38, of which 11 were waited for; matrix products, arithmetic and copies ran while one was open for 11% of the time, Pallas kernels for 7%

profile of v2, /device:TPU:0, one launch (start us, length us, event | category | flops | bytes accessed | tf_op | source)
XLA Modules:
  0.0 82.4 jit_solution(2416658874640685855)
XLA Ops:
  0.5 2.6 %collective-permute-start.4 = (bf16[64,1024]{1,0:T(8,128)(2,1)}, bf16[64,1024]{1,0:T(8,128)(2,1)S(1)}, u32[]{:S(2)}, u32[]{:S(2)}) collective-permute-start(bf16[64,1024]{1,0:T(8,128)(2,1)} %param.6), channel_id=1, source_target_pairs={{0,1},{1,0},{2,3},{3,2},{4,5},{5,4},{6,7},{7,6},{8,9},{9,8},{10,11... | collective-permute-start | bytes 393224 | tf_op jit(solution)/shard_map/ppermute | solution.py:73
  3.1 2.6 %collective-permute-start.9 = (bf16[64,1024]{1,0:T(8,128)(2,1)}, bf16[64,1024]{1,0:T(8,128)(2,1)S(1)}, u32[]{:S(2)}, u32[]{:S(2)}) collective-permute-start(bf16[64,1024]{1,0:T(8,128)(2,1)} %param.6), channel_id=1, source_target_pairs={{0,2},{1,3},{2,0},{3,1},{4,6},{5,7},{6,4},{7,5},{8,10},{9,11},{10,... | collective-permute-start | bytes 393224 | tf_op jit(solution)/shard_map/ppermute | solution.py:73
  6.5 2.4 %shard_map.65 = (bf16[384,1024]{1,0:T(8,128)(2,1)S(1)}, bf16[384,1024]{1,0:T(8,128)(2,1)S(1)}, bf16[384,1024]{1,0:T(8,128)(2,1)S(1)}, bf16[384,1024]{1,0:T(8,128)(2,1)S(1)}) custom-call(s32[4]{0:T(128)S(1)} %iota_xor_fusion.places_ref, bf16[1,384,4096]{2,1,0:T(8,128)(2,1)} %refs_0_.3), custom_call_target="tpu_custom_call" | custom-call | tf_op jit(solution)/shard_map/pallas_call | solution.py:121
  9.0 3.4 %shard_map.64 = (bf16[1024,768]{1,0:T(8,128)(2,1)S(1)}, bf16[1024,768]{1,0:T(8,128)(2,1)S(1)}, bf16[1024,768]{1,0:T(8,128)(2,1)S(1)}, bf16[1024,768]{1,0:T(8,128)(2,1)S(1)}) custom-call(s32[4]{0:T(128)S(1)} %iota_xor_fusion.places_ref, bf16[1,4096,384]{2,1,0:T(8,128)(2,1)} %refs_0_.2, bf16[1,4096,384]{2,1,0:T(8,128)(2,1)} %refs_1_.1), custom_call_target="tpu_custom_call" | custom-call | tf_op jit(solution)/shard_map/pallas_call | solution.py:121
  12.5 1.8 %collective-permute-start.1 = (bf16[128,1024]{1,0:T(8,128)(2,1)S(1)}, bf16[128,1024]{1,0:T(8,128)(2,1)S(1)}, u32[]{:S(2)}, u32[]{:S(2)}) collective-permute-start(bf16[128,1024]{1,0:T(8,128)(2,1)S(1)} %pad_maximum_fusion.6), channel_id=1, source_target_pairs={{0,8},{1,9},{2,10},{3,11},{4,20},{5,21},{6,22},{7,23},{8,0},{9,1},... | collective-permute-start | bytes 786440 | tf_op jit(solution)/shard_map/ppermute | solution.py:73
  16.3 1.6 %collective-permute-start.6 = (bf16[128,1024]{1,0:T(8,128)(2,1)S(1)}, bf16[128,1024]{1,0:T(8,128)(2,1)S(1)}, u32[]{:S(2)}, u32[]{:S(2)}) collective-permute-start(bf16[128,1024]{1,0:T(8,128)(2,1)S(1)} %pad_maximum_fusion.7), channel_id=1, source_target_pairs={{0,8},{1,9},{2,10},{3,11},{4,20},{5,21},{6,22},{7,23},{8,0},{9,1},... | collective-permute-start | bytes 786440 | tf_op jit(solution)/shard_map/ppermute | solution.py:73
  18.5 1.6 %collective-permute-start.11 = (bf16[128,1152]{1,0:T(8,128)(2,1)S(1)}, bf16[128,1152]{1,0:T(8,128)(2,1)S(1)}, u32[]{:S(2)}, u32[]{:S(2)}) collective-permute-start(bf16[128,1152]{1,0:T(8,128)(2,1)S(1)} %pad_maximum_fusion.5), channel_id=1, source_target_pairs={{0,8},{1,9},{2,10},{3,11},{4,20},{5,21},{6,22},{7,23},{8,0},{9,1},... | collective-permute-start | bytes 884744 | tf_op jit(solution)/shard_map/ppermute | solution.py:73
  20.1 1.6 %collective-permute-start.2 = (bf16[64,1024]{1,0:T(8,128)(2,1)S(1)}, bf16[64,1024]{1,0:T(8,128)(2,1)S(1)}, u32[]{:S(2)}, u32[]{:S(2)}) collective-permute-start(bf16[64,1024]{1,0:T(8,128)(2,1)S(1)} %slice.148), channel_id=1, source_target_pairs={{0,16},{1,17},{2,18},{3,19},{4,12},{5,13},{6,14},{7,15},{8,24},{9,... | collective-permute-start | bytes 393224 | tf_op jit(solution)/shard_map/ppermute | solution.py:73
  21.7 4.8 %collective-permute-done.2 = bf16[64,1024]{1,0:T(8,128)(2,1)S(1)} collective-permute-done((bf16[64,1024]{1,0:T(8,128)(2,1)S(1)}, bf16[64,1024]{1,0:T(8,128)(2,1)S(1)}, u32[]{:S(2)}, u32[]{:S(2)}) %collective-permute-start.2) | collective-permute-done | bytes 131104 | tf_op jit(solution)/shard_map/ppermute | solution.py:73
  26.7 1.6 %collective-permute-start.7 = (bf16[64,1024]{1,0:T(8,128)(2,1)S(1)}, bf16[64,1024]{1,0:T(8,128)(2,1)S(1)}, u32[]{:S(2)}, u32[]{:S(2)}) collective-permute-start(bf16[64,1024]{1,0:T(8,128)(2,1)S(1)} %slice.149), channel_id=1, source_target_pairs={{0,16},{1,17},{2,18},{3,19},{4,12},{5,13},{6,14},{7,15},{8,24},{9,... | collective-permute-start | bytes 393224 | tf_op jit(solution)/shard_map/ppermute | solution.py:73
  30.5 1.6 %collective-permute-start.12 = (bf16[64,1152]{1,0:T(8,128)(2,1)S(1)}, bf16[64,1152]{1,0:T(8,128)(2,1)S(1)}, u32[]{:S(2)}, u32[]{:S(2)}) collective-permute-start(bf16[64,1152]{1,0:T(8,128)(2,1)S(1)} %slice.150), channel_id=1, source_target_pairs={{0,16},{1,17},{2,18},{3,19},{4,12},{5,13},{6,14},{7,15},{8,24},{9,... | collective-permute-start | bytes 442376 | tf_op jit(solution)/shard_map/ppermute | solution.py:73
  33.4 2.2 %collective-permute-done.12 = bf16[64,1152]{1,0:T(8,128)(2,1)S(1)} collective-permute-done((bf16[64,1152]{1,0:T(8,128)(2,1)S(1)}, bf16[64,1152]{1,0:T(8,128)(2,1)S(1)}, u32[]{:S(2)}, u32[]{:S(2)}) %collective-permute-start.12) | collective-permute-done | bytes 147488 | tf_op jit(solution)/shard_map/ppermute | solution.py:73
  44.0 1.6 %collective-permute-start.20 = (bf16[64,1024]{1,0:T(8,128)(2,1)S(1)}, bf16[64,1024]{1,0:T(8,128)(2,1)S(1)}, u32[]{:S(2)}, u32[]{:S(2)}) collective-permute-start(bf16[64,1024]{1,0:T(8,128)(2,1)S(1)} %get-tuple-element.39), channel_id=1, source_target_pairs={{0,16},{1,17},{2,18},{3,19},{4,12},{5,13},{6,14},{7,15},{8,24},{9,... | collective-permute-start | bytes 393224 | tf_op jit(solution)/shard_map/ppermute | solution.py:73
  47.1 1.6 %collective-permute-start.29 = (bf16[64,1024]{1,0:T(8,128)(2,1)S(1)}, bf16[64,1024]{1,0:T(8,128)(2,1)S(1)}, u32[]{:S(2)}, u32[]{:S(2)}) collective-permute-start(bf16[64,1024]{1,0:T(8,128)(2,1)S(1)} %get-tuple-element.43), channel_id=1, source_target_pairs={{0,16},{1,17},{2,18},{3,19},{4,12},{5,13},{6,14},{7,15},{8,24},{9,... | collective-permute-start | bytes 393224 | tf_op jit(solution)/shard_map/ppermute | solution.py:73
  49.8 2.5 %collective-permute-start.21 = (bf16[128,1024]{1,0:T(8,128)(2,1)S(1)}, bf16[128,1024]{1,0:T(8,128)(2,1)S(1)}, u32[]{:S(2)}, u32[]{:S(2)}) collective-permute-start(bf16[128,1024]{1,0:T(8,128)(2,1)S(1)} %pad_maximum_fusion.9), channel_id=1, source_target_pairs={{0,8},{1,9},{2,10},{3,11},{4,20},{5,21},{6,22},{7,23},{8,0},{9,1},... | collective-permute-start | bytes 786440 | tf_op jit(solution)/shard_map/ppermute | solution.py:73
  52.4 1.3 %collective-permute-start.25 = (bf16[128,1024]{1,0:T(8,128)(2,1)S(1)}, bf16[128,1024]{1,0:T(8,128)(2,1)S(1)}, u32[]{:S(2)}, u32[]{:S(2)}) collective-permute-start(bf16[128,1024]{1,0:T(8,128)(2,1)S(1)} %pad_maximum_fusion.10), channel_id=1, source_target_pairs={{0,8},{1,9},{2,10},{3,11},{4,20},{5,21},{6,22},{7,23},{8,0},{9,1},... | collective-permute-start | bytes 786440 | tf_op jit(solution)/shard_map/ppermute | solution.py:73
  53.7 2.0 %collective-permute-start.30 = (bf16[128,1024]{1,0:T(8,128)(2,1)S(1)}, bf16[128,1024]{1,0:T(8,128)(2,1)S(1)}, u32[]{:S(2)}, u32[]{:S(2)}) collective-permute-start(bf16[128,1024]{1,0:T(8,128)(2,1)S(1)} %pad_maximum_fusion.11), channel_id=1, source_target_pairs={{0,8},{1,9},{2,10},{3,11},{4,20},{5,21},{6,22},{7,23},{8,0},{9,1},... | collective-permute-start | bytes 786440 | tf_op jit(solution)/shard_map/ppermute | solution.py:73
  55.8 2.7 %collective-permute-start.35 = (bf16[128,1024]{1,0:T(8,128)(2,1)S(1)}, bf16[128,1024]{1,0:T(8,128)(2,1)S(1)}, u32[]{:S(2)}, u32[]{:S(2)}) collective-permute-start(bf16[128,1024]{1,0:T(8,128)(2,1)S(1)} %pad_maximum_fusion.12), channel_id=1, source_target_pairs={{0,8},{1,9},{2,10},{3,11},{4,20},{5,21},{6,22},{7,23},{8,0},{9,1},... | collective-permute-start | bytes 786440 | tf_op jit(solution)/shard_map/ppermute | solution.py:73
  60.3 2.1 %collective-permute-done.30 = bf16[128,1024]{1,0:T(8,128)(2,1)S(1)} collective-permute-done((bf16[128,1024]{1,0:T(8,128)(2,1)S(1)}, bf16[128,1024]{1,0:T(8,128)(2,1)S(1)}, u32[]{:S(2)}, u32[]{:S(2)}) %collective-permute-start.30) | collective-permute-done | bytes 262176 | tf_op jit(solution)/shard_map/ppermute | solution.py:73
  62.6 2.7 %collective-permute-done.35 = bf16[128,1024]{1,0:T(8,128)(2,1)S(1)} collective-permute-done((bf16[128,1024]{1,0:T(8,128)(2,1)S(1)}, bf16[128,1024]{1,0:T(8,128)(2,1)S(1)}, u32[]{:S(2)}, u32[]{:S(2)}) %collective-permute-start.35) | collective-permute-done | bytes 262176 | tf_op jit(solution)/shard_map/ppermute | solution.py:73
  65.5 3.1 %collective-permute-start.27 = (bf16[64,1024]{1,0:T(8,128)(2,1)S(1)}, bf16[64,1024]{1,0:T(8,128)(2,1)S(1)}, u32[]{:S(2)}, u32[]{:S(2)}) collective-permute-start(bf16[64,1024]{1,0:T(8,128)(2,1)S(1)} %add_convert_fusion.9), channel_id=1, source_target_pairs={{0,1},{1,0},{2,3},{3,2},{4,5},{5,4},{6,7},{7,6},{8,9},{9,8},{10,11... | collective-permute-start | bytes 393224 | tf_op jit(solution)/shard_map/ppermute | solution.py:73
  69.8 1.5 %collective-permute-start.37 = (bf16[64,1024]{1,0:T(8,128)(2,1)S(1)}, bf16[64,1024]{1,0:T(8,128)(2,1)S(1)}, u32[]{:S(2)}, u32[]{:S(2)}) collective-permute-start(bf16[64,1024]{1,0:T(8,128)(2,1)S(1)} %add_convert_fusion.5), channel_id=1, source_target_pairs={{0,3},{1,2},{2,1},{3,0},{4,7},{5,6},{6,5},{7,4},{8,11},{9,10},{10,... | collective-permute-start | bytes 393224 | tf_op jit(solution)/shard_map/ppermute | solution.py:73
  71.3 3.4 %collective-permute-done.27 = bf16[64,1024]{1,0:T(8,128)(2,1)S(1)} collective-permute-done((bf16[64,1024]{1,0:T(8,128)(2,1)S(1)}, bf16[64,1024]{1,0:T(8,128)(2,1)S(1)}, u32[]{:S(2)}, u32[]{:S(2)}) %collective-permute-start.27) | collective-permute-done | bytes 131104 | tf_op jit(solution)/shard_map/ppermute | solution.py:73
  74.7 6.9 %collective-permute-done.32 = bf16[64,1024]{1,0:T(8,128)(2,1)S(1)} collective-permute-done((bf16[64,1024]{1,0:T(8,128)(2,1)S(1)}, bf16[64,1024]{1,0:T(8,128)(2,1)S(1)}, u32[]{:S(2)}, u32[]{:S(2)}) %collective-permute-start.32) | collective-permute-done | bytes 131104 | tf_op jit(solution)/shard_map/ppermute | solution.py:73
  (118 shorter events, 22.7 us)
Async XLA Ops:
  0.0 12.4 %collective-permute-start = (bf16[64,1024]{1,0:T(8,128)(2,1)}, bf16[64,1024]{1,0:T(8,128)(2,1)S(1)}, u32[]{:S(2)}, u32[]{:S(2)}) collective-permute-start(bf16[64,1024]{1,0:T(8,128)(2,1)} %param.6), channel_id=1, source_target_pairs={{0,4},{1,5},{2,6},{3,7},{4,0},{5,1},{6,2},{7,3},{8,12},{9,13},{10,... | collective-permute-start | bytes 393224 | tf_op jit(solution)/shard_map/ppermute | solution.py:73
  0.5 13.7 %collective-permute-start.4 = (bf16[64,1024]{1,0:T(8,128)(2,1)}, bf16[64,1024]{1,0:T(8,128)(2,1)S(1)}, u32[]{:S(2)}, u32[]{:S(2)}) collective-permute-start(bf16[64,1024]{1,0:T(8,128)(2,1)} %param.6), channel_id=1, source_target_pairs={{0,1},{1,0},{2,3},{3,2},{4,5},{5,4},{6,7},{7,6},{8,9},{9,8},{10,11... | collective-permute-start | bytes 393224 | tf_op jit(solution)/shard_map/ppermute | solution.py:73
  3.1 13.1 %collective-permute-start.9 = (bf16[64,1024]{1,0:T(8,128)(2,1)}, bf16[64,1024]{1,0:T(8,128)(2,1)S(1)}, u32[]{:S(2)}, u32[]{:S(2)}) collective-permute-start(bf16[64,1024]{1,0:T(8,128)(2,1)} %param.6), channel_id=1, source_target_pairs={{0,2},{1,3},{2,0},{3,1},{4,6},{5,7},{6,4},{7,5},{8,10},{9,11},{10,... | collective-permute-start | bytes 393224 | tf_op jit(solution)/shard_map/ppermute | solution.py:73
  5.6 9.7 %collective-permute-start.14 = (bf16[64,1024]{1,0:T(8,128)(2,1)}, bf16[64,1024]{1,0:T(8,128)(2,1)S(1)}, u32[]{:S(2)}, u32[]{:S(2)}) collective-permute-start(bf16[64,1024]{1,0:T(8,128)(2,1)} %param.6), channel_id=1, source_target_pairs={{0,3},{1,2},{2,1},{3,0},{4,7},{5,6},{6,5},{7,4},{8,11},{9,10},{10,... | collective-permute-start | bytes 393224 | tf_op jit(solution)/shard_map/ppermute | solution.py:73
  12.5 7.7 %collective-permute-start.1 = (bf16[128,1024]{1,0:T(8,128)(2,1)S(1)}, bf16[128,1024]{1,0:T(8,128)(2,1)S(1)}, u32[]{:S(2)}, u32[]{:S(2)}) collective-permute-start(bf16[128,1024]{1,0:T(8,128)(2,1)S(1)} %pad_maximum_fusion.6), channel_id=1, source_target_pairs={{0,8},{1,9},{2,10},{3,11},{4,20},{5,21},{6,22},{7,23},{8,0},{9,1},... | collective-permute-start | bytes 786440 | tf_op jit(solution)/shard_map/ppermute | solution.py:73
  16.3 10.3 %collective-permute-start.6 = (bf16[128,1024]{1,0:T(8,128)(2,1)S(1)}, bf16[128,1024]{1,0:T(8,128)(2,1)S(1)}, u32[]{:S(2)}, u32[]{:S(2)}) collective-permute-start(bf16[128,1024]{1,0:T(8,128)(2,1)S(1)} %pad_maximum_fusion.7), channel_id=1, source_target_pairs={{0,8},{1,9},{2,10},{3,11},{4,20},{5,21},{6,22},{7,23},{8,0},{9,1},... | collective-permute-start | bytes 786440 | tf_op jit(solution)/shard_map/ppermute | solution.py:73
  17.9 10.4 %collective-permute-start.16 = (bf16[128,1024]{1,0:T(8,128)(2,1)S(1)}, bf16[128,1024]{1,0:T(8,128)(2,1)S(1)}, u32[]{:S(2)}, u32[]{:S(2)}) collective-permute-start(bf16[128,1024]{1,0:T(8,128)(2,1)S(1)} %pad_maximum_fusion.8), channel_id=1, source_target_pairs={{0,8},{1,9},{2,10},{3,11},{4,20},{5,21},{6,22},{7,23},{8,0},{9,1},... | collective-permute-start | bytes 786440 | tf_op jit(solution)/shard_map/ppermute | solution.py:73
  18.5 11.9 %collective-permute-start.11 = (bf16[128,1152]{1,0:T(8,128)(2,1)S(1)}, bf16[128,1152]{1,0:T(8,128)(2,1)S(1)}, u32[]{:S(2)}, u32[]{:S(2)}) collective-permute-start(bf16[128,1152]{1,0:T(8,128)(2,1)S(1)} %pad_maximum_fusion.5), channel_id=1, source_target_pairs={{0,8},{1,9},{2,10},{3,11},{4,20},{5,21},{6,22},{7,23},{8,0},{9,1},... | collective-permute-start | bytes 884744 | tf_op jit(solution)/shard_map/ppermute | solution.py:73
  20.1 6.4 %collective-permute-start.2 = (bf16[64,1024]{1,0:T(8,128)(2,1)S(1)}, bf16[64,1024]{1,0:T(8,128)(2,1)S(1)}, u32[]{:S(2)}, u32[]{:S(2)}) collective-permute-start(bf16[64,1024]{1,0:T(8,128)(2,1)S(1)} %slice.148), channel_id=1, source_target_pairs={{0,16},{1,17},{2,18},{3,19},{4,12},{5,13},{6,14},{7,15},{8,24},{9,... | collective-permute-start | bytes 393224 | tf_op jit(solution)/shard_map/ppermute | solution.py:73
  26.6 9.3 %collective-permute-start.3 = (bf16[192,1024]{1,0:T(8,128)(2,1)S(1)}, bf16[192,1024]{1,0:T(8,128)(2,1)S(1)}, u32[]{:S(2)}, u32[]{:S(2)}) collective-permute-start(bf16[192,1024]{1,0:T(8,128)(2,1)S(1)} %pad_maximum_fusion.2), channel_id=1, source_target_pairs={{0,4},{1,5},{2,6},{3,7},{4,0},{5,1},{6,2},{7,3},{8,12},{9,13},{10,... | collective-permute-start | bytes 1179656 | tf_op jit(solution)/shard_map/ppermute | solution.py:73
  33.4 6.1 %collective-permute-start.18 = (bf16[192,1024]{1,0:T(8,128)(2,1)S(1)}, bf16[192,1024]{1,0:T(8,128)(2,1)S(1)}, u32[]{:S(2)}, u32[]{:S(2)}) collective-permute-start(bf16[192,1024]{1,0:T(8,128)(2,1)S(1)} %pad_maximum_fusion.4), channel_id=1, source_target_pairs={{0,4},{1,5},{2,6},{3,7},{4,0},{5,1},{6,2},{7,3},{8,12},{9,13},{10,... | collective-permute-start | bytes 1179656 | tf_op jit(solution)/shard_map/ppermute | solution.py:73
  44.0 5.7 %collective-permute-start.20 = (bf16[64,1024]{1,0:T(8,128)(2,1)S(1)}, bf16[64,1024]{1,0:T(8,128)(2,1)S(1)}, u32[]{:S(2)}, u32[]{:S(2)}) collective-permute-start(bf16[64,1024]{1,0:T(8,128)(2,1)S(1)} %get-tuple-element.39), channel_id=1, source_target_pairs={{0,16},{1,17},{2,18},{3,19},{4,12},{5,13},{6,14},{7,15},{8,24},{9,... | collective-permute-start | bytes 393224 | tf_op jit(solution)/shard_map/ppermute | solution.py:73
  46.0 6.3 %collective-permute-start.24 = (bf16[64,1024]{1,0:T(8,128)(2,1)S(1)}, bf16[64,1024]{1,0:T(8,128)(2,1)S(1)}, u32[]{:S(2)}, u32[]{:S(2)}) collective-permute-start(bf16[64,1024]{1,0:T(8,128)(2,1)S(1)} %get-tuple-element.41), channel_id=1, source_target_pairs={{0,16},{1,17},{2,18},{3,19},{4,12},{5,13},{6,14},{7,15},{8,24},{9,... | collective-permute-start | bytes 393224 | tf_op jit(solution)/shard_map/ppermute | solution.py:73
  47.1 6.6 %collective-permute-start.29 = (bf16[64,1024]{1,0:T(8,128)(2,1)S(1)}, bf16[64,1024]{1,0:T(8,128)(2,1)S(1)}, u32[]{:S(2)}, u32[]{:S(2)}) collective-permute-start(bf16[64,1024]{1,0:T(8,128)(2,1)S(1)} %get-tuple-element.43), channel_id=1, source_target_pairs={{0,16},{1,17},{2,18},{3,19},{4,12},{5,13},{6,14},{7,15},{8,24},{9,... | collective-permute-start | bytes 393224 | tf_op jit(solution)/shard_map/ppermute | solution.py:73
  49.1 6.6 %collective-permute-start.34 = (bf16[64,1024]{1,0:T(8,128)(2,1)S(1)}, bf16[64,1024]{1,0:T(8,128)(2,1)S(1)}, u32[]{:S(2)}, u32[]{:S(2)}) collective-permute-start(bf16[64,1024]{1,0:T(8,128)(2,1)S(1)} %get-tuple-element.45), channel_id=1, source_target_pairs={{0,16},{1,17},{2,18},{3,19},{4,12},{5,13},{6,14},{7,15},{8,24},{9,... | collective-permute-start | bytes 393224 | tf_op jit(solution)/shard_map/ppermute | solution.py:73
  49.8 10.0 %collective-permute-start.21 = (bf16[128,1024]{1,0:T(8,128)(2,1)S(1)}, bf16[128,1024]{1,0:T(8,128)(2,1)S(1)}, u32[]{:S(2)}, u32[]{:S(2)}) collective-permute-start(bf16[128,1024]{1,0:T(8,128)(2,1)S(1)} %pad_maximum_fusion.9), channel_id=1, source_target_pairs={{0,8},{1,9},{2,10},{3,11},{4,20},{5,21},{6,22},{7,23},{8,0},{9,1},... | collective-permute-start | bytes 786440 | tf_op jit(solution)/shard_map/ppermute | solution.py:73
  52.4 7.3 %collective-permute-start.25 = (bf16[128,1024]{1,0:T(8,128)(2,1)S(1)}, bf16[128,1024]{1,0:T(8,128)(2,1)S(1)}, u32[]{:S(2)}, u32[]{:S(2)}) collective-permute-start(bf16[128,1024]{1,0:T(8,128)(2,1)S(1)} %pad_maximum_fusion.10), channel_id=1, source_target_pairs={{0,8},{1,9},{2,10},{3,11},{4,20},{5,21},{6,22},{7,23},{8,0},{9,1},... | collective-permute-start | bytes 786440 | tf_op jit(solution)/shard_map/ppermute | solution.py:73
  53.7 8.8 %collective-permute-start.30 = (bf16[128,1024]{1,0:T(8,128)(2,1)S(1)}, bf16[128,1024]{1,0:T(8,128)(2,1)S(1)}, u32[]{:S(2)}, u32[]{:S(2)}) collective-permute-start(bf16[128,1024]{1,0:T(8,128)(2,1)S(1)} %pad_maximum_fusion.11), channel_id=1, source_target_pairs={{0,8},{1,9},{2,10},{3,11},{4,20},{5,21},{6,22},{7,23},{8,0},{9,1},... | collective-permute-start | bytes 786440 | tf_op jit(solution)/shard_map/ppermute | solution.py:73
  55.8 9.5 %collective-permute-start.35 = (bf16[128,1024]{1,0:T(8,128)(2,1)S(1)}, bf16[128,1024]{1,0:T(8,128)(2,1)S(1)}, u32[]{:S(2)}, u32[]{:S(2)}) collective-permute-start(bf16[128,1024]{1,0:T(8,128)(2,1)S(1)} %pad_maximum_fusion.12), channel_id=1, source_target_pairs={{0,8},{1,9},{2,10},{3,11},{4,20},{5,21},{6,22},{7,23},{8,0},{9,1},... | collective-permute-start | bytes 786440 | tf_op jit(solution)/shard_map/ppermute | solution.py:73
  59.8 11.5 %collective-permute-start.22 = (bf16[64,1024]{1,0:T(8,128)(2,1)S(1)}, bf16[64,1024]{1,0:T(8,128)(2,1)S(1)}, u32[]{:S(2)}, u32[]{:S(2)}) collective-permute-start(bf16[64,1024]{1,0:T(8,128)(2,1)S(1)} %slice.160), channel_id=1, source_target_pairs={{0,4},{1,5},{2,6},{3,7},{4,0},{5,1},{6,2},{7,3},{8,12},{9,13},{10,... | collective-permute-start | bytes 393224 | tf_op jit(solution)/shard_map/ppermute | solution.py:73
  62.5 6.1 %collective-permute-start.31 = (bf16[64,1024]{1,0:T(8,128)(2,1)S(1)}, bf16[64,1024]{1,0:T(8,128)(2,1)S(1)}, u32[]{:S(2)}, u32[]{:S(2)}) collective-permute-start(bf16[64,1024]{1,0:T(8,128)(2,1)S(1)} %slice.172), channel_id=1, source_target_pairs={{0,4},{1,5},{2,6},{3,7},{4,0},{5,1},{6,2},{7,3},{8,12},{9,13},{10,... | collective-permute-start | bytes 393224 | tf_op jit(solution)/shard_map/ppermute | solution.py:73
  65.5 9.3 %collective-permute-start.27 = (bf16[64,1024]{1,0:T(8,128)(2,1)S(1)}, bf16[64,1024]{1,0:T(8,128)(2,1)S(1)}, u32[]{:S(2)}, u32[]{:S(2)}) collective-permute-start(bf16[64,1024]{1,0:T(8,128)(2,1)S(1)} %add_convert_fusion.9), channel_id=1, source_target_pairs={{0,1},{1,0},{2,3},{3,2},{4,5},{5,4},{6,7},{7,6},{8,9},{9,8},{10,11... | collective-permute-start | bytes 393224 | tf_op jit(solution)/shard_map/ppermute | solution.py:73
  68.6 13.0 %collective-permute-start.32 = (bf16[64,1024]{1,0:T(8,128)(2,1)S(1)}, bf16[64,1024]{1,0:T(8,128)(2,1)S(1)}, u32[]{:S(2)}, u32[]{:S(2)}) collective-permute-start(bf16[64,1024]{1,0:T(8,128)(2,1)S(1)} %add_convert_fusion.7), channel_id=1, source_target_pairs={{0,2},{1,3},{2,0},{3,1},{4,6},{5,7},{6,4},{7,5},{8,10},{9,11},{10,... | collective-permute-start | bytes 393224 | tf_op jit(solution)/shard_map/ppermute | solution.py:73
  69.8 11.9 %collective-permute-start.37 = (bf16[64,1024]{1,0:T(8,128)(2,1)S(1)}, bf16[64,1024]{1,0:T(8,128)(2,1)S(1)}, u32[]{:S(2)}, u32[]{:S(2)}) collective-permute-start(bf16[64,1024]{1,0:T(8,128)(2,1)S(1)} %add_convert_fusion.5), channel_id=1, source_target_pairs={{0,3},{1,2},{2,1},{3,0},{4,7},{5,6},{6,5},{7,4},{8,11},{9,10},{10,... | collective-permute-start | bytes 393224 | tf_op jit(solution)/shard_map/ppermute | solution.py:73
  (15 other events, 59.9 us)

commit v3 on v2

--- a/solution.py
+++ b/solution.py
@@ -9,6 +9,8 @@
 IN_CHUNKS = [[0], [1], [2], [3]]
 OUT_CHUNKS = [[3], [2], [1], [0]]
 TERMS_IN = 2
+IN_DIRECT = (0, 1, 2, 3)
+OUT_DIRECT = (0, 1, 2, 3)
 
 
 def slot_plan(tokens, expert_ids, gate_weights, w_gate, w_up, w_down):
@@ -85,6 +87,10 @@
     return toward(a, lambda e, z: (e ^ (4 >> (e & 1)), z))
 
 
+def corner(a):
+    return toward(a, lambda e, z: (e ^ 6, z))
+
+
 def along(a, k):
     return toward(a, lambda e, z: (e, z ^ k))
 
@@ -129,25 +135,31 @@
     )(places, *[pltpu.with_memory_space_constraint(a, pltpu.HBM) for a in sources])
 
 
-def spread(a):
+def spread(a, tag):
     rows = a.shape[0]
     pair = core_pair(a)
     side = first_side(jnp.concatenate([a, pair], axis=0))
-    far = second_side(side[:rows])
+    far = corner(a) if int(tag) in IN_DIRECT else second_side(side[:rows])
     brought = jnp.concatenate([side, far], axis=0)
     swapped = core_pair(brought)
     return jnp.concatenate([a, brought], axis=0), jnp.concatenate([pair, swapped], axis=0)
 
 
-def collect(mine_of, other_of):
+def collect(mine_of, other_of, tag):
     got = core_pair(half(other_of()))
     part = half(mine_of() + f32(got))
     rows = part.shape[0] // 4
+    own = part[:rows]
+    if int(tag) in OUT_DIRECT:
+        far = corner(part[3 * rows :])
+        side = first_side(part[rows : 3 * rows])
+        swapped = core_pair(side[rows:])
+        return f32(own) + f32(far) + f32(side[:rows]) + f32(swapped)
     far = second_side(part[3 * rows :])
     near = half(f32(part[rows : 2 * rows]) + f32(far))
     side = first_side(jnp.concatenate([near, part[2 * rows : 3 * rows]], axis=0))
     swapped = core_pair(side[rows:])
-    return f32(part[:rows]) + f32(side[:rows]) + f32(swapped)
+    return f32(own) + f32(side[:rows]) + f32(swapped)
 
 
 def gather_plan(tokens, expert_ids, gate_weights, w_gate, w_up, w_down):
@@ -175,7 +187,7 @@
         parts = [tokens if k == 0 else zs[k] for k in ks]
         if n == TERMS_IN:
             parts.append(terms)
-        both = spread(jnp.concatenate(parts, axis=1) if len(parts) > 1 else parts[0])
+        both = spread(jnp.concatenate(parts, axis=1) if len(parts) > 1 else parts[0], str(n))
         for i, k in enumerate(ks):
             for h in range(2):
                 acc[h] = acc[h] + jnp.dot(
@@ -194,14 +206,14 @@
         half(jax.nn.silu(a[:, :units]) * a[:, units:] * w[:, None]) for a, w in zip(acc, weight)
     ]
     sums = {}
-    for ks in OUT_CHUNKS:
+    for n, ks in enumerate(OUT_CHUNKS):
         def product(h):
             return jnp.concatenate(
                 [jnp.dot(hidden[h], downs[k], preferred_element_type=jnp.float32) for k in ks],
                 axis=1,
             )
 
-        total = collect(lambda: product(0), lambda: product(1))
+        total = collect(lambda: product(0), lambda: product(1), str(n))
         for i, k in enumerate(ks):
             sums[k] = total[:, i * cols : (i + 1) * cols]
             if k:

time: 82.6 us -> 89.8 us (1.087)
  waiting for transfers between devices: 27.6 us -> 41.8 us
  starting transfers between devices: 37.5 us -> 30.6 us
    ppermute x38, waiting for transfers between devices: 27.6 us -> 41.8 us  [toward(): return lax.ppermute(a, ('expert', 'tensor'), pairs)]
    ppermute x38, starting transfers between devices: 37.5 us -> 30.6 us  [toward(): return lax.ppermute(a, ('expert', 'tensor'), pairs)]
  transfers between devices with their start and end apart: 38 -> 38, of which waited for: 11 -> 13; matrix products, arithmetic and copies ran while one was open for 11% -> 10% of each run, Pallas kernels for 7% -> 7%
where the time goes in v3:
time: 89.8 us; the launch traced here: 89.6 us
  waiting for transfers between devices  41.8 us (47%)
  starting transfers between devices  30.6 us (34%)
  matrix products  8.09 us (9%)
  Pallas kernels  5.84 us (7%)
  other arithmetic  2.41 us (3%)
    ppermute x38, waiting for transfers between devices, toward(): return lax.ppermute(a, ('expert', 'tensor'), pairs)  41.8 us
    ppermute x38, starting transfers between devices, toward(): return lax.ppermute(a, ('expert', 'tensor'), pairs)  30.6 us
    pallas_call x2, Pallas kernels, load_slices(): pl.pallas_call(kernel, out_shape=[out] * count, in_specs=[pl.BlockSpec(me...  5.84 us
    dot_general x8, matrix products, gather_plan(): jnp.dot(both[h][:, i * cols:(i + 1) * cols], pairs[k], preferred_element_...  4.57 us
    dot_general x8, matrix products, product(): jnp.dot(hidden[h], downs[k], preferred_element_type=jnp.float32)  3.52 us
  transfers between devices with their start and end apart: 38, of which 13 were waited for; matrix products, arithmetic and copies ran while one was open for 10% of the time, Pallas kernels for 7%

profile of v3, /device:TPU:0, one launch (start us, length us, event | category | flops | bytes accessed | tf_op | source)
XLA Modules:
  0.0 89.6 jit_solution(3597529994024585927)
XLA Ops:
  0.5 3.4 %collective-permute-start.2 = (bf16[64,1024]{1,0:T(8,128)(2,1)}, bf16[64,1024]{1,0:T(8,128)(2,1)S(1)}, u32[]{:S(2)}, u32[]{:S(2)}) collective-permute-start(bf16[64,1024]{1,0:T(8,128)(2,1)} %param.6), channel_id=1, source_target_pairs={{0,24},{1,25},{2,26},{3,27},{4,28},{5,29},{6,30},{7,31},{8,16},{9,... | collective-permute-start | bytes 393224 | tf_op jit(solution)/shard_map/ppermute | solution.py:75
  3.9 1.6 %collective-permute-start.4 = (bf16[64,1024]{1,0:T(8,128)(2,1)}, bf16[64,1024]{1,0:T(8,128)(2,1)S(1)}, u32[]{:S(2)}, u32[]{:S(2)}) collective-permute-start(bf16[64,1024]{1,0:T(8,128)(2,1)} %param.6), channel_id=1, source_target_pairs={{0,1},{1,0},{2,3},{3,2},{4,5},{5,4},{6,7},{7,6},{8,9},{9,8},{10,11... | collective-permute-start | bytes 393224 | tf_op jit(solution)/shard_map/ppermute | solution.py:75
  5.5 2.6 %collective-permute-start.9 = (bf16[64,1024]{1,0:T(8,128)(2,1)}, bf16[64,1024]{1,0:T(8,128)(2,1)S(1)}, u32[]{:S(2)}, u32[]{:S(2)}) collective-permute-start(bf16[64,1024]{1,0:T(8,128)(2,1)} %param.6), channel_id=1, source_target_pairs={{0,2},{1,3},{2,0},{3,1},{4,6},{5,7},{6,4},{7,5},{8,10},{9,11},{10,... | collective-permute-start | bytes 393224 | tf_op jit(solution)/shard_map/ppermute | solution.py:75
  9.2 2.4 %shard_map.65 = (bf16[384,1024]{1,0:T(8,128)(2,1)S(1)}, bf16[384,1024]{1,0:T(8,128)(2,1)S(1)}, bf16[384,1024]{1,0:T(8,128)(2,1)S(1)}, bf16[384,1024]{1,0:T(8,128)(2,1)S(1)}) custom-call(s32[4]{0:T(128)S(1)} %iota_xor_fusion.places_ref, bf16[1,384,4096]{2,1,0:T(8,128)(2,1)} %refs_0_.3), custom_call_target="tpu_custom_call" | custom-call | tf_op jit(solution)/shard_map/pallas_call | solution.py:127
  11.6 3.4 %shard_map.64 = (bf16[1024,768]{1,0:T(8,128)(2,1)S(1)}, bf16[1024,768]{1,0:T(8,128)(2,1)S(1)}, bf16[1024,768]{1,0:T(8,128)(2,1)S(1)}, bf16[1024,768]{1,0:T(8,128)(2,1)S(1)}) custom-call(s32[4]{0:T(128)S(1)} %iota_xor_fusion.places_ref, bf16[1,4096,384]{2,1,0:T(8,128)(2,1)} %refs_0_.2, bf16[1,4096,384]{2,1,0:T(8,128)(2,1)} %refs_1_.1), custom_call_target="tpu_custom_call" | custom-call | tf_op jit(solution)/shard_map/pallas_call | solution.py:127
  15.7 1.8 %collective-permute-done.14 = bf16[64,1024]{1,0:T(8,128)(2,1)S(1)} collective-permute-done((bf16[64,1024]{1,0:T(8,128)(2,1)}, bf16[64,1024]{1,0:T(8,128)(2,1)S(1)}, u32[]{:S(2)}, u32[]{:S(2)}) %collective-permute-start.14) | collective-permute-done | bytes 131104 | tf_op jit(solution)/shard_map/ppermute | solution.py:75
  19.3 2.5 %collective-permute-start.17 = (bf16[64,1024]{1,0:T(8,128)(2,1)S(1)}, bf16[64,1024]{1,0:T(8,128)(2,1)S(1)}, u32[]{:S(2)}, u32[]{:S(2)}) collective-permute-start(bf16[64,1024]{1,0:T(8,128)(2,1)S(1)} %collective-permute-done.14), channel_id=1, source_target_pairs={{0,24},{1,25},{2,26},{3,27},{4,28},{5,29},{6,30},{7,31},{8,16},{9,... | collective-permute-start | bytes 393224 | tf_op jit(solution)/shard_map/ppermute | solution.py:75
  22.5 1.6 %collective-permute-start.16 = (bf16[128,1024]{1,0:T(8,128)(2,1)S(1)}, bf16[128,1024]{1,0:T(8,128)(2,1)S(1)}, u32[]{:S(2)}, u32[]{:S(2)}) collective-permute-start(bf16[128,1024]{1,0:T(8,128)(2,1)S(1)} %pad_maximum_fusion.8), channel_id=1, source_target_pairs={{0,8},{1,9},{2,10},{3,11},{4,20},{5,21},{6,22},{7,23},{8,0},{9,1},... | collective-permute-start | bytes 786440 | tf_op jit(solution)/shard_map/ppermute | solution.py:75
  26.7 5.1 %collective-permute-done.6 = bf16[128,1024]{1,0:T(8,128)(2,1)S(1)} collective-permute-done((bf16[128,1024]{1,0:T(8,128)(2,1)S(1)}, bf16[128,1024]{1,0:T(8,128)(2,1)S(1)}, u32[]{:S(2)}, u32[]{:S(2)}) %collective-permute-start.6) | collective-permute-done | bytes 262176 | tf_op jit(solution)/shard_map/ppermute | solution.py:75
  32.9 1.7 %collective-permute-done.16 = bf16[128,1024]{1,0:T(8,128)(2,1)S(1)} collective-permute-done((bf16[128,1024]{1,0:T(8,128)(2,1)S(1)}, bf16[128,1024]{1,0:T(8,128)(2,1)S(1)}, u32[]{:S(2)}, u32[]{:S(2)}) %collective-permute-start.16) | collective-permute-done | bytes 262176 | tf_op jit(solution)/shard_map/ppermute | solution.py:75
  34.6 1.1 %collective-permute-start.18 = (bf16[192,1024]{1,0:T(8,128)(2,1)S(1)}, bf16[192,1024]{1,0:T(8,128)(2,1)S(1)}, u32[]{:S(2)}, u32[]{:S(2)}) collective-permute-start(bf16[192,1024]{1,0:T(8,128)(2,1)S(1)} %pad_maximum_fusion.4), channel_id=1, source_target_pairs={{0,4},{1,5},{2,6},{3,7},{4,0},{5,1},{6,2},{7,3},{8,12},{9,13},{10,... | collective-permute-start | bytes 1179656 | tf_op jit(solution)/shard_map/ppermute | solution.py:75
  35.7 4.6 %collective-permute-done.12 = bf16[64,1152]{1,0:T(8,128)(2,1)S(1)} collective-permute-done((bf16[64,1152]{1,0:T(8,128)(2,1)S(1)}, bf16[64,1152]{1,0:T(8,128)(2,1)S(1)}, u32[]{:S(2)}, u32[]{:S(2)}) %collective-permute-start.12) | collective-permute-done | bytes 147488 | tf_op jit(solution)/shard_map/ppermute | solution.py:75
  49.7 1.5 %collective-permute-start.25 = (bf16[128,1024]{1,0:T(8,128)(2,1)S(1)}, bf16[128,1024]{1,0:T(8,128)(2,1)S(1)}, u32[]{:S(2)}, u32[]{:S(2)}) collective-permute-start(bf16[128,1024]{1,0:T(8,128)(2,1)S(1)} %slice.126), channel_id=1, source_target_pairs={{0,8},{1,9},{2,10},{3,11},{4,20},{5,21},{6,22},{7,23},{8,0},{9,1},... | collective-permute-start | bytes 786440 | tf_op jit(solution)/shard_map/ppermute | solution.py:75
  52.8 1.5 %collective-permute-start.35 = (bf16[128,1024]{1,0:T(8,128)(2,1)S(1)}, bf16[128,1024]{1,0:T(8,128)(2,1)S(1)}, u32[]{:S(2)}, u32[]{:S(2)}) collective-permute-start(bf16[128,1024]{1,0:T(8,128)(2,1)S(1)} %slice.136), channel_id=1, source_target_pairs={{0,8},{1,9},{2,10},{3,11},{4,20},{5,21},{6,22},{7,23},{8,0},{9,1},... | collective-permute-start | bytes 786440 | tf_op jit(solution)/shard_map/ppermute | solution.py:75
  54.9 4.4 %collective-permute-done.25 = bf16[128,1024]{1,0:T(8,128)(2,1)S(1)} collective-permute-done((bf16[128,1024]{1,0:T(8,128)(2,1)S(1)}, bf16[128,1024]{1,0:T(8,128)(2,1)S(1)}, u32[]{:S(2)}, u32[]{:S(2)}) %collective-permute-start.25) | collective-permute-done | bytes 262176 | tf_op jit(solution)/shard_map/ppermute | solution.py:75
  59.5 3.0 %collective-permute-done.30 = bf16[128,1024]{1,0:T(8,128)(2,1)S(1)} collective-permute-done((bf16[128,1024]{1,0:T(8,128)(2,1)S(1)}, bf16[128,1024]{1,0:T(8,128)(2,1)S(1)}, u32[]{:S(2)}, u32[]{:S(2)}) %collective-permute-start.30) | collective-permute-done | bytes 262176 | tf_op jit(solution)/shard_map/ppermute | solution.py:75
  62.6 5.1 %collective-permute-done.35 = bf16[128,1024]{1,0:T(8,128)(2,1)S(1)} collective-permute-done((bf16[128,1024]{1,0:T(8,128)(2,1)S(1)}, bf16[128,1024]{1,0:T(8,128)(2,1)S(1)}, u32[]{:S(2)}, u32[]{:S(2)}) %collective-permute-start.35) | collective-permute-done | bytes 262176 | tf_op jit(solution)/shard_map/ppermute | solution.py:75
  67.7 1.3 %collective-permute-done.24 = bf16[64,1024]{1,0:T(8,128)(2,1)S(1)} collective-permute-done((bf16[64,1024]{1,0:T(8,128)(2,1)S(1)}, bf16[64,1024]{1,0:T(8,128)(2,1)S(1)}, u32[]{:S(2)}, u32[]{:S(2)}) %collective-permute-start.24) | collective-permute-done | bytes 131104 | tf_op jit(solution)/shard_map/ppermute | solution.py:75
  69.6 3.7 %collective-permute-done.29 = bf16[64,1024]{1,0:T(8,128)(2,1)S(1)} collective-permute-done((bf16[64,1024]{1,0:T(8,128)(2,1)S(1)}, bf16[64,1024]{1,0:T(8,128)(2,1)S(1)}, u32[]{:S(2)}, u32[]{:S(2)}) %collective-permute-start.29) | collective-permute-done | bytes 131104 | tf_op jit(solution)/shard_map/ppermute | solution.py:75
  73.2 2.5 %collective-permute-start.27 = (bf16[64,1024]{1,0:T(8,128)(2,1)S(1)}, bf16[64,1024]{1,0:T(8,128)(2,1)S(1)}, u32[]{:S(2)}, u32[]{:S(2)}) collective-permute-start(bf16[64,1024]{1,0:T(8,128)(2,1)S(1)} %add_convert_fusion.7), channel_id=1, source_target_pairs={{0,1},{1,0},{2,3},{3,2},{4,5},{5,4},{6,7},{7,6},{8,9},{9,8},{10,11... | collective-permute-start | bytes 393224 | tf_op jit(solution)/shard_map/ppermute | solution.py:75
  75.8 2.3 %collective-permute-start.32 = (bf16[64,1024]{1,0:T(8,128)(2,1)S(1)}, bf16[64,1024]{1,0:T(8,128)(2,1)S(1)}, u32[]{:S(2)}, u32[]{:S(2)}) collective-permute-start(bf16[64,1024]{1,0:T(8,128)(2,1)S(1)} %add_convert_fusion.6), channel_id=1, source_target_pairs={{0,2},{1,3},{2,0},{3,1},{4,6},{5,7},{6,4},{7,5},{8,10},{9,11},{10,... | collective-permute-start | bytes 393224 | tf_op jit(solution)/shard_map/ppermute | solution.py:75
  78.2 1.4 %collective-permute-start.37 = (bf16[64,1024]{1,0:T(8,128)(2,1)S(1)}, bf16[64,1024]{1,0:T(8,128)(2,1)S(1)}, u32[]{:S(2)}, u32[]{:S(2)}) collective-permute-start(bf16[64,1024]{1,0:T(8,128)(2,1)S(1)} %add_convert_fusion.5), channel_id=1, source_target_pairs={{0,3},{1,2},{2,1},{3,0},{4,7},{5,6},{6,5},{7,4},{8,11},{9,10},{10,... | collective-permute-start | bytes 393224 | tf_op jit(solution)/shard_map/ppermute | solution.py:75
  79.7 2.4 %collective-permute-done.27 = bf16[64,1024]{1,0:T(8,128)(2,1)S(1)} collective-permute-done((bf16[64,1024]{1,0:T(8,128)(2,1)S(1)}, bf16[64,1024]{1,0:T(8,128)(2,1)S(1)}, u32[]{:S(2)}, u32[]{:S(2)}) %collective-permute-start.27) | collective-permute-done | bytes 131104 | tf_op jit(solution)/shard_map/ppermute | solution.py:75
  82.0 6.8 %collective-permute-done.32 = bf16[64,1024]{1,0:T(8,128)(2,1)S(1)} collective-permute-done((bf16[64,1024]{1,0:T(8,128)(2,1)S(1)}, bf16[64,1024]{1,0:T(8,128)(2,1)S(1)}, u32[]{:S(2)}, u32[]{:S(2)}) %collective-permute-start.32) | collective-permute-done | bytes 131104 | tf_op jit(solution)/shard_map/ppermute | solution.py:75
  (110 shorter events, 21.5 us)
Async XLA Ops:
  0.0 15.1 %collective-permute-start = (bf16[64,1024]{1,0:T(8,128)(2,1)}, bf16[64,1024]{1,0:T(8,128)(2,1)S(1)}, u32[]{:S(2)}, u32[]{:S(2)}) collective-permute-start(bf16[64,1024]{1,0:T(8,128)(2,1)} %param.6), channel_id=1, source_target_pairs={{0,4},{1,5},{2,6},{3,7},{4,0},{5,1},{6,2},{7,3},{8,12},{9,13},{10,... | collective-permute-start | bytes 393224 | tf_op jit(solution)/shard_map/ppermute | solution.py:75
  0.5 22.0 %collective-permute-start.2 = (bf16[64,1024]{1,0:T(8,128)(2,1)}, bf16[64,1024]{1,0:T(8,128)(2,1)S(1)}, u32[]{:S(2)}, u32[]{:S(2)}) collective-permute-start(bf16[64,1024]{1,0:T(8,128)(2,1)} %param.6), channel_id=1, source_target_pairs={{0,24},{1,25},{2,26},{3,27},{4,28},{5,29},{6,30},{7,31},{8,16},{9,... | collective-permute-start | bytes 393224 | tf_op jit(solution)/shard_map/ppermute | solution.py:75
  3.9 11.8 %collective-permute-start.4 = (bf16[64,1024]{1,0:T(8,128)(2,1)}, bf16[64,1024]{1,0:T(8,128)(2,1)S(1)}, u32[]{:S(2)}, u32[]{:S(2)}) collective-permute-start(bf16[64,1024]{1,0:T(8,128)(2,1)} %param.6), channel_id=1, source_target_pairs={{0,1},{1,0},{2,3},{3,2},{4,5},{5,4},{6,7},{7,6},{8,9},{9,8},{10,11... | collective-permute-start | bytes 393224 | tf_op jit(solution)/shard_map/ppermute | solution.py:75
  5.5 13.1 %collective-permute-start.9 = (bf16[64,1024]{1,0:T(8,128)(2,1)}, bf16[64,1024]{1,0:T(8,128)(2,1)S(1)}, u32[]{:S(2)}, u32[]{:S(2)}) collective-permute-start(bf16[64,1024]{1,0:T(8,128)(2,1)} %param.6), channel_id=1, source_target_pairs={{0,2},{1,3},{2,0},{3,1},{4,6},{5,7},{6,4},{7,5},{8,10},{9,11},{10,... | collective-permute-start | bytes 393224 | tf_op jit(solution)/shard_map/ppermute | solution.py:75
  8.1 9.4 %collective-permute-start.14 = (bf16[64,1024]{1,0:T(8,128)(2,1)}, bf16[64,1024]{1,0:T(8,128)(2,1)S(1)}, u32[]{:S(2)}, u32[]{:S(2)}) collective-permute-start(bf16[64,1024]{1,0:T(8,128)(2,1)} %param.6), channel_id=1, source_target_pairs={{0,3},{1,2},{2,1},{3,0},{4,7},{5,6},{6,5},{7,4},{8,11},{9,10},{10,... | collective-permute-start | bytes 393224 | tf_op jit(solution)/shard_map/ppermute | solution.py:75
  15.1 8.9 %collective-permute-start.1 = (bf16[128,1024]{1,0:T(8,128)(2,1)S(1)}, bf16[128,1024]{1,0:T(8,128)(2,1)S(1)}, u32[]{:S(2)}, u32[]{:S(2)}) collective-permute-start(bf16[128,1024]{1,0:T(8,128)(2,1)S(1)} %pad_maximum_fusion.6), channel_id=1, source_target_pairs={{0,8},{1,9},{2,10},{3,11},{4,20},{5,21},{6,22},{7,23},{8,0},{9,1},... | collective-permute-start | bytes 786440 | tf_op jit(solution)/shard_map/ppermute | solution.py:75
  19.3 13.6 %collective-permute-start.17 = (bf16[64,1024]{1,0:T(8,128)(2,1)S(1)}, bf16[64,1024]{1,0:T(8,128)(2,1)S(1)}, u32[]{:S(2)}, u32[]{:S(2)}) collective-permute-start(bf16[64,1024]{1,0:T(8,128)(2,1)S(1)} %collective-permute-done.14), channel_id=1, source_target_pairs={{0,24},{1,25},{2,26},{3,27},{4,28},{5,29},{6,30},{7,31},{8,16},{9,... | collective-permute-start | bytes 393224 | tf_op jit(solution)/shard_map/ppermute | solution.py:75
  21.8 10.0 %collective-permute-start.6 = (bf16[128,1024]{1,0:T(8,128)(2,1)S(1)}, bf16[128,1024]{1,0:T(8,128)(2,1)S(1)}, u32[]{:S(2)}, u32[]{:S(2)}) collective-permute-start(bf16[128,1024]{1,0:T(8,128)(2,1)S(1)} %pad_maximum_fusion.7), channel_id=1, source_target_pairs={{0,8},{1,9},{2,10},{3,11},{4,20},{5,21},{6,22},{7,23},{8,0},{9,1},... | collective-permute-start | bytes 786440 | tf_op jit(solution)/shard_map/ppermute | solution.py:75
  22.5 12.1 %collective-permute-start.16 = (bf16[128,1024]{1,0:T(8,128)(2,1)S(1)}, bf16[128,1024]{1,0:T(8,128)(2,1)S(1)}, u32[]{:S(2)}, u32[]{:S(2)}) collective-permute-start(bf16[128,1024]{1,0:T(8,128)(2,1)S(1)} %pad_maximum_fusion.8), channel_id=1, source_target_pairs={{0,8},{1,9},{2,10},{3,11},{4,20},{5,21},{6,22},{7,23},{8,0},{9,1},... | collective-permute-start | bytes 786440 | tf_op jit(solution)/shard_map/ppermute | solution.py:75
  24.0 16.2 %collective-permute-start.11 = (bf16[128,1152]{1,0:T(8,128)(2,1)S(1)}, bf16[128,1152]{1,0:T(8,128)(2,1)S(1)}, u32[]{:S(2)}, u32[]{:S(2)}) collective-permute-start(bf16[128,1152]{1,0:T(8,128)(2,1)S(1)} %pad_maximum_fusion.5), channel_id=1, source_target_pairs={{0,8},{1,9},{2,10},{3,11},{4,20},{5,21},{6,22},{7,23},{8,0},{9,1},... | collective-permute-start | bytes 884744 | tf_op jit(solution)/shard_map/ppermute | solution.py:75
  26.1 14.1 %collective-permute-start.12 = (bf16[64,1152]{1,0:T(8,128)(2,1)S(1)}, bf16[64,1152]{1,0:T(8,128)(2,1)S(1)}, u32[]{:S(2)}, u32[]{:S(2)}) collective-permute-start(bf16[64,1152]{1,0:T(8,128)(2,1)S(1)} %pad_maximum_fusion.9), channel_id=1, source_target_pairs={{0,24},{1,25},{2,26},{3,27},{4,28},{5,29},{6,30},{7,31},{8,16},{9,... | collective-permute-start | bytes 442376 | tf_op jit(solution)/shard_map/ppermute | solution.py:75
  32.9 8.8 %collective-permute-start.8 = (bf16[192,1024]{1,0:T(8,128)(2,1)S(1)}, bf16[192,1024]{1,0:T(8,128)(2,1)S(1)}, u32[]{:S(2)}, u32[]{:S(2)}) collective-permute-start(bf16[192,1024]{1,0:T(8,128)(2,1)S(1)} %pad_maximum_fusion.3), channel_id=1, source_target_pairs={{0,4},{1,5},{2,6},{3,7},{4,0},{5,1},{6,2},{7,3},{8,12},{9,13},{10,... | collective-permute-start | bytes 1179656 | tf_op jit(solution)/shard_map/ppermute | solution.py:75
  34.6 9.4 %collective-permute-start.18 = (bf16[192,1024]{1,0:T(8,128)(2,1)S(1)}, bf16[192,1024]{1,0:T(8,128)(2,1)S(1)}, u32[]{:S(2)}, u32[]{:S(2)}) collective-permute-start(bf16[192,1024]{1,0:T(8,128)(2,1)S(1)} %pad_maximum_fusion.4), channel_id=1, source_target_pairs={{0,4},{1,5},{2,6},{3,7},{4,0},{5,1},{6,2},{7,3},{8,12},{9,13},{10,... | collective-permute-start | bytes 1179656 | tf_op jit(solution)/shard_map/ppermute | solution.py:75
  48.6 10.8 %collective-permute-start.21 = (bf16[128,1024]{1,0:T(8,128)(2,1)S(1)}, bf16[128,1024]{1,0:T(8,128)(2,1)S(1)}, u32[]{:S(2)}, u32[]{:S(2)}) collective-permute-start(bf16[128,1024]{1,0:T(8,128)(2,1)S(1)} %slice.121), channel_id=1, source_target_pairs={{0,8},{1,9},{2,10},{3,11},{4,20},{5,21},{6,22},{7,23},{8,0},{9,1},... | collective-permute-start | bytes 786440 | tf_op jit(solution)/shard_map/ppermute | solution.py:75
  49.7 9.6 %collective-permute-start.25 = (bf16[128,1024]{1,0:T(8,128)(2,1)S(1)}, bf16[128,1024]{1,0:T(8,128)(2,1)S(1)}, u32[]{:S(2)}, u32[]{:S(2)}) collective-permute-start(bf16[128,1024]{1,0:T(8,128)(2,1)S(1)} %slice.126), channel_id=1, source_target_pairs={{0,8},{1,9},{2,10},{3,11},{4,20},{5,21},{6,22},{7,23},{8,0},{9,1},... | collective-permute-start | bytes 786440 | tf_op jit(solution)/shard_map/ppermute | solution.py:75
  51.7 10.8 %collective-permute-start.30 = (bf16[128,1024]{1,0:T(8,128)(2,1)S(1)}, bf16[128,1024]{1,0:T(8,128)(2,1)S(1)}, u32[]{:S(2)}, u32[]{:S(2)}) collective-permute-start(bf16[128,1024]{1,0:T(8,128)(2,1)S(1)} %slice.131), channel_id=1, source_target_pairs={{0,8},{1,9},{2,10},{3,11},{4,20},{5,21},{6,22},{7,23},{8,0},{9,1},... | collective-permute-start | bytes 786440 | tf_op jit(solution)/shard_map/ppermute | solution.py:75
  52.8 14.9 %collective-permute-start.35 = (bf16[128,1024]{1,0:T(8,128)(2,1)S(1)}, bf16[128,1024]{1,0:T(8,128)(2,1)S(1)}, u32[]{:S(2)}, u32[]{:S(2)}) collective-permute-start(bf16[128,1024]{1,0:T(8,128)(2,1)S(1)} %slice.136), channel_id=1, source_target_pairs={{0,8},{1,9},{2,10},{3,11},{4,20},{5,21},{6,22},{7,23},{8,0},{9,1},... | collective-permute-start | bytes 786440 | tf_op jit(solution)/shard_map/ppermute | solution.py:75
  54.3 14.6 %collective-permute-start.24 = (bf16[64,1024]{1,0:T(8,128)(2,1)S(1)}, bf16[64,1024]{1,0:T(8,128)(2,1)S(1)}, u32[]{:S(2)}, u32[]{:S(2)}) collective-permute-start(bf16[64,1024]{1,0:T(8,128)(2,1)S(1)} %slice.125), channel_id=1, source_target_pairs={{0,24},{1,25},{2,26},{3,27},{4,28},{5,29},{6,30},{7,31},{8,16},{9,... | collective-permute-start | bytes 393224 | tf_op jit(solution)/shard_map/ppermute | solution.py:75
  59.3 9.7 %collective-permute-start.26 = (bf16[64,1024]{1,0:T(8,128)(2,1)S(1)}, bf16[64,1024]{1,0:T(8,128)(2,1)S(1)}, u32[]{:S(2)}, u32[]{:S(2)}) collective-permute-start(bf16[64,1024]{1,0:T(8,128)(2,1)S(1)} %slice.128), channel_id=1, source_target_pairs={{0,4},{1,5},{2,6},{3,7},{4,0},{5,1},{6,2},{7,3},{8,12},{9,13},{10,... | collective-permute-start | bytes 393224 | tf_op jit(solution)/shard_map/ppermute | solution.py:75
  59.4 20.3 %collective-permute-start.20 = (bf16[64,1024]{1,0:T(8,128)(2,1)S(1)}, bf16[64,1024]{1,0:T(8,128)(2,1)S(1)}, u32[]{:S(2)}, u32[]{:S(2)}) collective-permute-start(bf16[64,1024]{1,0:T(8,128)(2,1)S(1)} %slice.120), channel_id=1, source_target_pairs={{0,24},{1,25},{2,26},{3,27},{4,28},{5,29},{6,30},{7,31},{8,16},{9,... | collective-permute-start | bytes 393224 | tf_op jit(solution)/shard_map/ppermute | solution.py:75
  62.5 10.7 %collective-permute-start.29 = (bf16[64,1024]{1,0:T(8,128)(2,1)S(1)}, bf16[64,1024]{1,0:T(8,128)(2,1)S(1)}, u32[]{:S(2)}, u32[]{:S(2)}) collective-permute-start(bf16[64,1024]{1,0:T(8,128)(2,1)S(1)} %slice.130), channel_id=1, source_target_pairs={{0,24},{1,25},{2,26},{3,27},{4,28},{5,29},{6,30},{7,31},{8,16},{9,... | collective-permute-start | bytes 393224 | tf_op jit(solution)/shard_map/ppermute | solution.py:75
  69.0 10.7 %collective-permute-start.22 = (bf16[64,1024]{1,0:T(8,128)(2,1)S(1)}, bf16[64,1024]{1,0:T(8,128)(2,1)S(1)}, u32[]{:S(2)}, u32[]{:S(2)}) collective-permute-start(bf16[64,1024]{1,0:T(8,128)(2,1)S(1)} %slice.123), channel_id=1, source_target_pairs={{0,4},{1,5},{2,6},{3,7},{4,0},{5,1},{6,2},{7,3},{8,12},{9,13},{10,... | collective-permute-start | bytes 393224 | tf_op jit(solution)/shard_map/ppermute | solution.py:75
  75.8 13.0 %collective-permute-start.32 = (bf16[64,1024]{1,0:T(8,128)(2,1)S(1)}, bf16[64,1024]{1,0:T(8,128)(2,1)S(1)}, u32[]{:S(2)}, u32[]{:S(2)}) collective-permute-start(bf16[64,1024]{1,0:T(8,128)(2,1)S(1)} %add_convert_fusion.6), channel_id=1, source_target_pairs={{0,2},{1,3},{2,0},{3,1},{4,6},{5,7},{6,4},{7,5},{8,10},{9,11},{10,... | collective-permute-start | bytes 393224 | tf_op jit(solution)/shard_map/ppermute | solution.py:75
  78.2 10.6 %collective-permute-start.37 = (bf16[64,1024]{1,0:T(8,128)(2,1)S(1)}, bf16[64,1024]{1,0:T(8,128)(2,1)S(1)}, u32[]{:S(2)}, u32[]{:S(2)}) collective-permute-start(bf16[64,1024]{1,0:T(8,128)(2,1)S(1)} %add_convert_fusion.5), channel_id=1, source_target_pairs={{0,3},{1,2},{2,1},{3,0},{4,7},{5,6},{6,5},{7,4},{8,11},{9,10},{10,... | collective-permute-start | bytes 393224 | tf_op jit(solution)/shard_map/ppermute | solution.py:75
  (15 other events, 70.5 us)

commit v4 on v3

--- a/solution.py
+++ b/solution.py
@@ -9,6 +9,7 @@
 IN_CHUNKS = [[0], [1], [2], [3]]
 OUT_CHUNKS = [[3], [2], [1], [0]]
 TERMS_IN = 2
+SPLIT = (3,)
 IN_DIRECT = (0, 1, 2, 3)
 OUT_DIRECT = (0, 1, 2, 3)
 
@@ -146,15 +147,23 @@
 
 
 def collect(mine_of, other_of, tag):
-    got = core_pair(half(other_of()))
-    part = half(mine_of() + f32(got))
-    rows = part.shape[0] // 4
-    own = part[:rows]
+    got = core_pair(half(other_of(0, None)))
+    rows = got.shape[0] // 4
     if int(tag) in OUT_DIRECT:
-        far = corner(part[3 * rows :])
-        side = first_side(part[rows : 3 * rows])
+        cut = 3 * rows
+        if int(tag) in SPLIT:
+            near = half(mine_of(rows, cut) + f32(got[rows:cut]))
+            last = half(mine_of(cut, None) + f32(got[cut:]))
+            own = mine_of(0, rows) + f32(got[:rows])
+        else:
+            part = half(mine_of(0, None) + f32(got))
+            own, near, last = part[:rows], part[rows:cut], part[cut:]
+        far = corner(last)
+        side = first_side(near)
         swapped = core_pair(side[rows:])
         return f32(own) + f32(far) + f32(side[:rows]) + f32(swapped)
+    part = half(mine_of(0, None) + f32(got))
+    own = part[:rows]
     far = second_side(part[3 * rows :])
     near = half(f32(part[rows : 2 * rows]) + f32(far))
     side = first_side(jnp.concatenate([near, part[2 * rows : 3 * rows]], axis=0))
@@ -205,22 +214,29 @@
     hidden = [
         half(jax.nn.silu(a[:, :units]) * a[:, units:] * w[:, None]) for a, w in zip(acc, weight)
     ]
-    sums = {}
+    sums, passed = {}, {}
     for n, ks in enumerate(OUT_CHUNKS):
-        def product(h):
+        def product(h, start, stop):
             return jnp.concatenate(
-                [jnp.dot(hidden[h], downs[k], preferred_element_type=jnp.float32) for k in ks],
+                [jnp.dot(hidden[h][start:stop], downs[k], preferred_element_type=jnp.float32)
+                    for k in ks
+                ],
                 axis=1,
             )
 
-        total = collect(lambda: product(0), lambda: product(1), str(n))
+        total = collect(lambda *rows: product(0, *rows), lambda *rows: product(1, *rows), str(n))
         for i, k in enumerate(ks):
             sums[k] = total[:, i * cols : (i + 1) * cols]
+            if k ^ 2 in passed:
+                sums[k] = sums[k] + f32(passed[k ^ 2])
             if k:
                 sums[k] = half(sums[k])
+            if k > 2:
+                passed[k] = along(sums[k], 2)
     mixed = sums[0]
     for k in range(1, shards):
-        mixed = mixed + f32(along(sums[k], k))
+        if k not in passed:
+            mixed = mixed + f32(along(sums[k], k))
     return half(mixed)
 
 

time: 89.8 us -> 94.6 us (1.053)
  waiting for transfers between devices: 41.8 us -> 45.3 us
    ppermute x38, waiting for transfers between devices: 41.8 us -> 45.3 us  [toward(): return lax.ppermute(a, ('expert', 'tensor'), pairs)]
    dot_general x8 -> x10, matrix products: 3.52 us -> 3.91 us  [product(): jnp.dot(hidden[h][start:stop], downs[k], preferred_element_type=jnp.float32)]
  transfers between devices with their start and end apart: 38 -> 38, of which waited for: 13 -> 12; matrix products, arithmetic and copies ran while one was open for 10% -> 10% of each run, Pallas kernels for 7% -> 6%
where the time goes in v4:
time: 94.6 us; the launch traced here: 94.4 us
  waiting for transfers between devices  45.3 us (48%)
  starting transfers between devices  31.5 us (33%)
  matrix products  8.48 us (9%)
  Pallas kernels  5.84 us (6%)
  other arithmetic  2.42 us (3%)
    ppermute x38, waiting for transfers between devices, toward(): return lax.ppermute(a, ('expert', 'tensor'), pairs)  45.3 us
    ppermute x38, starting transfers between devices, toward(): return lax.ppermute(a, ('expert', 'tensor'), pairs)  31.5 us
    pallas_call x2, Pallas kernels, load_slices(): pl.pallas_call(kernel, out_shape=[out] * count, in_specs=[pl.BlockSpec(me...  5.84 us
    dot_general x8, matrix products, gather_plan(): jnp.dot(both[h][:, i * cols:(i + 1) * cols], pairs[k], preferred_element_...  4.57 us
    dot_general x10, matrix products, product(): jnp.dot(hidden[h][start:stop], downs[k], preferred_element_type=jnp.float32)  3.91 us
  transfers between devices with their start and end apart: 38, of which 12 were waited for; matrix products, arithmetic and copies ran while one was open for 10% of the time, Pallas kernels for 6%

profile of v4, /device:TPU:0, one launch (start us, length us, event | category | flops | bytes accessed | tf_op | source)
XLA Modules:
  0.0 94.4 jit_solution(1780371349511149600)
XLA Ops:
  0.5 3.4 %collective-permute-start.2 = (bf16[64,1024]{1,0:T(8,128)(2,1)}, bf16[64,1024]{1,0:T(8,128)(2,1)S(1)}, u32[]{:S(2)}, u32[]{:S(2)}) collective-permute-start(bf16[64,1024]{1,0:T(8,128)(2,1)} %param.6), channel_id=1, source_target_pairs={{0,24},{1,25},{2,26},{3,27},{4,28},{5,29},{6,30},{7,31},{8,16},{9,... | collective-permute-start | bytes 393224 | tf_op jit(solution)/shard_map/ppermute | solution.py:76
  3.9 1.6 %collective-permute-start.4 = (bf16[64,1024]{1,0:T(8,128)(2,1)}, bf16[64,1024]{1,0:T(8,128)(2,1)S(1)}, u32[]{:S(2)}, u32[]{:S(2)}) collective-permute-start(bf16[64,1024]{1,0:T(8,128)(2,1)} %param.6), channel_id=1, source_target_pairs={{0,1},{1,0},{2,3},{3,2},{4,5},{5,4},{6,7},{7,6},{8,9},{9,8},{10,11... | collective-permute-start | bytes 393224 | tf_op jit(solution)/shard_map/ppermute | solution.py:76
  5.5 2.6 %collective-permute-start.9 = (bf16[64,1024]{1,0:T(8,128)(2,1)}, bf16[64,1024]{1,0:T(8,128)(2,1)S(1)}, u32[]{:S(2)}, u32[]{:S(2)}) collective-permute-start(bf16[64,1024]{1,0:T(8,128)(2,1)} %param.6), channel_id=1, source_target_pairs={{0,2},{1,3},{2,0},{3,1},{4,6},{5,7},{6,4},{7,5},{8,10},{9,11},{10,... | collective-permute-start | bytes 393224 | tf_op jit(solution)/shard_map/ppermute | solution.py:76
  9.2 2.4 %shard_map.65 = (bf16[384,1024]{1,0:T(8,128)(2,1)S(1)}, bf16[384,1024]{1,0:T(8,128)(2,1)S(1)}, bf16[384,1024]{1,0:T(8,128)(2,1)S(1)}, bf16[384,1024]{1,0:T(8,128)(2,1)S(1)}) custom-call(s32[4]{0:T(128)S(1)} %iota_xor_fusion.places_ref, bf16[1,384,4096]{2,1,0:T(8,128)(2,1)} %refs_0_.3), custom_call_target="tpu_custom_call" | custom-call | tf_op jit(solution)/shard_map/pallas_call | solution.py:128
  11.6 3.4 %shard_map.64 = (bf16[1024,768]{1,0:T(8,128)(2,1)S(1)}, bf16[1024,768]{1,0:T(8,128)(2,1)S(1)}, bf16[1024,768]{1,0:T(8,128)(2,1)S(1)}, bf16[1024,768]{1,0:T(8,128)(2,1)S(1)}) custom-call(s32[4]{0:T(128)S(1)} %iota_xor_fusion.places_ref, bf16[1,4096,384]{2,1,0:T(8,128)(2,1)} %refs_0_.2, bf16[1,4096,384]{2,1,0:T(8,128)(2,1)} %refs_1_.1), custom_call_target="tpu_custom_call" | custom-call | tf_op jit(solution)/shard_map/pallas_call | solution.py:128
  15.7 1.8 %collective-permute-done.14 = bf16[64,1024]{1,0:T(8,128)(2,1)S(1)} collective-permute-done((bf16[64,1024]{1,0:T(8,128)(2,1)}, bf16[64,1024]{1,0:T(8,128)(2,1)S(1)}, u32[]{:S(2)}, u32[]{:S(2)}) %collective-permute-start.14) | collective-permute-done | bytes 131104 | tf_op jit(solution)/shard_map/ppermute | solution.py:76
  17.5 1.1 %collective-permute-done.9 = bf16[64,1024]{1,0:T(8,128)(2,1)S(1)} collective-permute-done((bf16[64,1024]{1,0:T(8,128)(2,1)}, bf16[64,1024]{1,0:T(8,128)(2,1)S(1)}, u32[]{:S(2)}, u32[]{:S(2)}) %collective-permute-start.9) | collective-permute-done | bytes 131104 | tf_op jit(solution)/shard_map/ppermute | solution.py:76
  19.3 2.5 %collective-permute-start.17 = (bf16[64,1024]{1,0:T(8,128)(2,1)S(1)}, bf16[64,1024]{1,0:T(8,128)(2,1)S(1)}, u32[]{:S(2)}, u32[]{:S(2)}) collective-permute-start(bf16[64,1024]{1,0:T(8,128)(2,1)S(1)} %collective-permute-done.14), channel_id=1, source_target_pairs={{0,24},{1,25},{2,26},{3,27},{4,28},{5,29},{6,30},{7,31},{8,16},{9,... | collective-permute-start | bytes 393224 | tf_op jit(solution)/shard_map/ppermute | solution.py:76
  22.5 1.6 %collective-permute-start.16 = (bf16[128,1024]{1,0:T(8,128)(2,1)S(1)}, bf16[128,1024]{1,0:T(8,128)(2,1)S(1)}, u32[]{:S(2)}, u32[]{:S(2)}) collective-permute-start(bf16[128,1024]{1,0:T(8,128)(2,1)S(1)} %pad_maximum_fusion.8), channel_id=1, source_target_pairs={{0,8},{1,9},{2,10},{3,11},{4,20},{5,21},{6,22},{7,23},{8,0},{9,1},... | collective-permute-start | bytes 786440 | tf_op jit(solution)/shard_map/ppermute | solution.py:76
  25.2 0.9 %collective-permute-done.7 = bf16[64,1024]{1,0:T(8,128)(2,1)S(1)} collective-permute-done((bf16[64,1024]{1,0:T(8,128)(2,1)S(1)}, bf16[64,1024]{1,0:T(8,128)(2,1)S(1)}, u32[]{:S(2)}, u32[]{:S(2)}) %collective-permute-start.7) | collective-permute-done | bytes 131104 | tf_op jit(solution)/shard_map/ppermute | solution.py:76
  26.7 5.1 %collective-permute-done.6 = bf16[128,1024]{1,0:T(8,128)(2,1)S(1)} collective-permute-done((bf16[128,1024]{1,0:T(8,128)(2,1)S(1)}, bf16[128,1024]{1,0:T(8,128)(2,1)S(1)}, u32[]{:S(2)}, u32[]{:S(2)}) %collective-permute-start.6) | collective-permute-done | bytes 262176 | tf_op jit(solution)/shard_map/ppermute | solution.py:76
  31.8 1.0 %collective-permute-start.3 = (bf16[192,1024]{1,0:T(8,128)(2,1)S(1)}, bf16[192,1024]{1,0:T(8,128)(2,1)S(1)}, u32[]{:S(2)}, u32[]{:S(2)}) collective-permute-start(bf16[192,1024]{1,0:T(8,128)(2,1)S(1)} %pad_maximum_fusion.2), channel_id=1, source_target_pairs={{0,4},{1,5},{2,6},{3,7},{4,0},{5,1},{6,2},{7,3},{8,12},{9,13},{10,... | collective-permute-start | bytes 1179656 | tf_op jit(solution)/shard_map/ppermute | solution.py:76
  32.9 1.7 %collective-permute-done.16 = bf16[128,1024]{1,0:T(8,128)(2,1)S(1)} collective-permute-done((bf16[128,1024]{1,0:T(8,128)(2,1)S(1)}, bf16[128,1024]{1,0:T(8,128)(2,1)S(1)}, u32[]{:S(2)}, u32[]{:S(2)}) %collective-permute-start.16) | collective-permute-done | bytes 262176 | tf_op jit(solution)/shard_map/ppermute | solution.py:76
  34.6 1.1 %collective-permute-start.18 = (bf16[192,1024]{1,0:T(8,128)(2,1)S(1)}, bf16[192,1024]{1,0:T(8,128)(2,1)S(1)}, u32[]{:S(2)}, u32[]{:S(2)}) collective-permute-start(bf16[192,1024]{1,0:T(8,128)(2,1)S(1)} %pad_maximum_fusion.4), channel_id=1, source_target_pairs={{0,4},{1,5},{2,6},{3,7},{4,0},{5,1},{6,2},{7,3},{8,12},{9,13},{10,... | collective-permute-start | bytes 1179656 | tf_op jit(solution)/shard_map/ppermute | solution.py:76
  35.7 4.6 %collective-permute-done.12 = bf16[64,1152]{1,0:T(8,128)(2,1)S(1)} collective-permute-done((bf16[64,1152]{1,0:T(8,128)(2,1)S(1)}, bf16[64,1152]{1,0:T(8,128)(2,1)S(1)}, u32[]{:S(2)}, u32[]{:S(2)}) %collective-permute-start.12) | collective-permute-done | bytes 147488 | tf_op jit(solution)/shard_map/ppermute | solution.py:76
  49.5 1.5 %collective-permute-start.25 = (bf16[128,1024]{1,0:T(8,128)(2,1)S(1)}, bf16[128,1024]{1,0:T(8,128)(2,1)S(1)}, u32[]{:S(2)}, u32[]{:S(2)}) collective-permute-start(bf16[128,1024]{1,0:T(8,128)(2,1)S(1)} %slice.141), channel_id=1, source_target_pairs={{0,8},{1,9},{2,10},{3,11},{4,20},{5,21},{6,22},{7,23},{8,0},{9,1},... | collective-permute-start | bytes 786440 | tf_op jit(solution)/shard_map/ppermute | solution.py:76
  52.6 1.5 %collective-permute-start.35 = (bf16[128,1024]{1,0:T(8,128)(2,1)S(1)}, bf16[128,1024]{1,0:T(8,128)(2,1)S(1)}, u32[]{:S(2)}, u32[]{:S(2)}) collective-permute-start(bf16[128,1024]{1,0:T(8,128)(2,1)S(1)} %slice.151), channel_id=1, source_target_pairs={{0,8},{1,9},{2,10},{3,11},{4,20},{5,21},{6,22},{7,23},{8,0},{9,1},... | collective-permute-start | bytes 786440 | tf_op jit(solution)/shard_map/ppermute | solution.py:76
  54.8 7.1 %collective-permute-done.29 = bf16[128,1024]{1,0:T(8,128)(2,1)S(1)} collective-permute-done((bf16[128,1024]{1,0:T(8,128)(2,1)S(1)}, bf16[128,1024]{1,0:T(8,128)(2,1)S(1)}, u32[]{:S(2)}, u32[]{:S(2)}) %collective-permute-start.29) | collective-permute-done | bytes 262176 | tf_op jit(solution)/shard_map/ppermute | solution.py:76
  62.8 2.5 %collective-permute-start.24 = (bf16[64,1024]{1,0:T(8,128)(2,1)S(1)}, bf16[64,1024]{1,0:T(8,128)(2,1)S(1)}, u32[]{:S(2)}, u32[]{:S(2)}) collective-permute-start(bf16[64,1024]{1,0:T(8,128)(2,1)S(1)} %slice.140), channel_id=1, source_target_pairs={{0,24},{1,25},{2,26},{3,27},{4,28},{5,29},{6,30},{7,31},{8,16},{9,... | collective-permute-start | bytes 393224 | tf_op jit(solution)/shard_map/ppermute | solution.py:76
  66.6 8.1 %collective-permute-done.34 = bf16[64,1024]{1,0:T(8,128)(2,1)S(1)} collective-permute-done((bf16[64,1024]{1,0:T(8,128)(2,1)S(1)}, bf16[64,1024]{1,0:T(8,128)(2,1)S(1)}, u32[]{:S(2)}, u32[]{:S(2)}) %collective-permute-start.34) | collective-permute-done | bytes 131104 | tf_op jit(solution)/shard_map/ppermute | solution.py:76
  74.8 3.5 %collective-permute-start.31 = (bf16[64,1024]{1,0:T(8,128)(2,1)S(1)}, bf16[64,1024]{1,0:T(8,128)(2,1)S(1)}, u32[]{:S(2)}, u32[]{:S(2)}) collective-permute-start(bf16[64,1024]{1,0:T(8,128)(2,1)S(1)} %add_convert_fusion.7), channel_id=1, source_target_pairs={{0,2},{1,3},{2,0},{3,1},{4,6},{5,7},{6,4},{7,5},{8,10},{9,11},{10,... | collective-permute-start | bytes 393224 | tf_op jit(solution)/shard_map/ppermute | solution.py:76
  78.4 9.8 %collective-permute-done.31 = bf16[64,1024]{1,0:T(8,128)(2,1)S(1)} collective-permute-done((bf16[64,1024]{1,0:T(8,128)(2,1)S(1)}, bf16[64,1024]{1,0:T(8,128)(2,1)S(1)}, u32[]{:S(2)}, u32[]{:S(2)}) %collective-permute-start.31) | collective-permute-done | bytes 131104 | tf_op jit(solution)/shard_map/ppermute | solution.py:76
  88.7 2.2 %collective-permute-done.37 = bf16[64,1024]{1,0:T(8,128)(2,1)S(1)} collective-permute-done((bf16[64,1024]{1,0:T(8,128)(2,1)S(1)}, bf16[64,1024]{1,0:T(8,128)(2,1)S(1)}, u32[]{:S(2)}, u32[]{:S(2)}) %collective-permute-start.37) | collective-permute-done | bytes 131104 | tf_op jit(solution)/shard_map/ppermute | solution.py:76
  90.9 2.8 %collective-permute-done.32 = bf16[64,1024]{1,0:T(8,128)(2,1)S(1)} collective-permute-done((bf16[64,1024]{1,0:T(8,128)(2,1)S(1)}, bf16[64,1024]{1,0:T(8,128)(2,1)S(1)}, u32[]{:S(2)}, u32[]{:S(2)}) %collective-permute-start.32) | collective-permute-done | bytes 131104 | tf_op jit(solution)/shard_map/ppermute | solution.py:76
  (110 shorter events, 20.0 us)
Async XLA Ops:
  0.0 15.1 %collective-permute-start = (bf16[64,1024]{1,0:T(8,128)(2,1)}, bf16[64,1024]{1,0:T(8,128)(2,1)S(1)}, u32[]{:S(2)}, u32[]{:S(2)}) collective-permute-start(bf16[64,1024]{1,0:T(8,128)(2,1)} %param.6), channel_id=1, source_target_pairs={{0,4},{1,5},{2,6},{3,7},{4,0},{5,1},{6,2},{7,3},{8,12},{9,13},{10,... | collective-permute-start | bytes 393224 | tf_op jit(solution)/shard_map/ppermute | solution.py:76
  0.5 22.0 %collective-permute-start.2 = (bf16[64,1024]{1,0:T(8,128)(2,1)}, bf16[64,1024]{1,0:T(8,128)(2,1)S(1)}, u32[]{:S(2)}, u32[]{:S(2)}) collective-permute-start(bf16[64,1024]{1,0:T(8,128)(2,1)} %param.6), channel_id=1, source_target_pairs={{0,24},{1,25},{2,26},{3,27},{4,28},{5,29},{6,30},{7,31},{8,16},{9,... | collective-permute-start | bytes 393224 | tf_op jit(solution)/shard_map/ppermute | solution.py:76
  3.9 11.8 %collective-permute-start.4 = (bf16[64,1024]{1,0:T(8,128)(2,1)}, bf16[64,1024]{1,0:T(8,128)(2,1)S(1)}, u32[]{:S(2)}, u32[]{:S(2)}) collective-permute-start(bf16[64,1024]{1,0:T(8,128)(2,1)} %param.6), channel_id=1, source_target_pairs={{0,1},{1,0},{2,3},{3,2},{4,5},{5,4},{6,7},{7,6},{8,9},{9,8},{10,11... | collective-permute-start | bytes 393224 | tf_op jit(solution)/shard_map/ppermute | solution.py:76
  5.5 13.1 %collective-permute-start.9 = (bf16[64,1024]{1,0:T(8,128)(2,1)}, bf16[64,1024]{1,0:T(8,128)(2,1)S(1)}, u32[]{:S(2)}, u32[]{:S(2)}) collective-permute-start(bf16[64,1024]{1,0:T(8,128)(2,1)} %param.6), channel_id=1, source_target_pairs={{0,2},{1,3},{2,0},{3,1},{4,6},{5,7},{6,4},{7,5},{8,10},{9,11},{10,... | collective-permute-start | bytes 393224 | tf_op jit(solution)/shard_map/ppermute | solution.py:76
  8.1 9.4 %collective-permute-start.14 = (bf16[64,1024]{1,0:T(8,128)(2,1)}, bf16[64,1024]{1,0:T(8,128)(2,1)S(1)}, u32[]{:S(2)}, u32[]{:S(2)}) collective-permute-start(bf16[64,1024]{1,0:T(8,128)(2,1)} %param.6), channel_id=1, source_target_pairs={{0,3},{1,2},{2,1},{3,0},{4,7},{5,6},{6,5},{7,4},{8,11},{9,10},{10,... | collective-permute-start | bytes 393224 | tf_op jit(solution)/shard_map/ppermute | solution.py:76
  15.1 8.9 %collective-permute-start.1 = (bf16[128,1024]{1,0:T(8,128)(2,1)S(1)}, bf16[128,1024]{1,0:T(8,128)(2,1)S(1)}, u32[]{:S(2)}, u32[]{:S(2)}) collective-permute-start(bf16[128,1024]{1,0:T(8,128)(2,1)S(1)} %pad_maximum_fusion.6), channel_id=1, source_target_pairs={{0,8},{1,9},{2,10},{3,11},{4,20},{5,21},{6,22},{7,23},{8,0},{9,1},... | collective-permute-start | bytes 786440 | tf_op jit(solution)/shard_map/ppermute | solution.py:76
  19.3 13.6 %collective-permute-start.17 = (bf16[64,1024]{1,0:T(8,128)(2,1)S(1)}, bf16[64,1024]{1,0:T(8,128)(2,1)S(1)}, u32[]{:S(2)}, u32[]{:S(2)}) collective-permute-start(bf16[64,1024]{1,0:T(8,128)(2,1)S(1)} %collective-permute-done.14), channel_id=1, source_target_pairs={{0,24},{1,25},{2,26},{3,27},{4,28},{5,29},{6,30},{7,31},{8,16},{9,... | collective-permute-start | bytes 393224 | tf_op jit(solution)/shard_map/ppermute | solution.py:76
  21.8 10.0 %collective-permute-start.6 = (bf16[128,1024]{1,0:T(8,128)(2,1)S(1)}, bf16[128,1024]{1,0:T(8,128)(2,1)S(1)}, u32[]{:S(2)}, u32[]{:S(2)}) collective-permute-start(bf16[128,1024]{1,0:T(8,128)(2,1)S(1)} %pad_maximum_fusion.7), channel_id=1, source_target_pairs={{0,8},{1,9},{2,10},{3,11},{4,20},{5,21},{6,22},{7,23},{8,0},{9,1},... | collective-permute-start | bytes 786440 | tf_op jit(solution)/shard_map/ppermute | solution.py:76
  22.5 12.1 %collective-permute-start.16 = (bf16[128,1024]{1,0:T(8,128)(2,1)S(1)}, bf16[128,1024]{1,0:T(8,128)(2,1)S(1)}, u32[]{:S(2)}, u32[]{:S(2)}) collective-permute-start(bf16[128,1024]{1,0:T(8,128)(2,1)S(1)} %pad_maximum_fusion.8), channel_id=1, source_target_pairs={{0,8},{1,9},{2,10},{3,11},{4,20},{5,21},{6,22},{7,23},{8,0},{9,1},... | collective-permute-start | bytes 786440 | tf_op jit(solution)/shard_map/ppermute | solution.py:76
  24.0 16.2 %collective-permute-start.11 = (bf16[128,1152]{1,0:T(8,128)(2,1)S(1)}, bf16[128,1152]{1,0:T(8,128)(2,1)S(1)}, u32[]{:S(2)}, u32[]{:S(2)}) collective-permute-start(bf16[128,1152]{1,0:T(8,128)(2,1)S(1)} %pad_maximum_fusion.5), channel_id=1, source_target_pairs={{0,8},{1,9},{2,10},{3,11},{4,20},{5,21},{6,22},{7,23},{8,0},{9,1},... | collective-permute-start | bytes 884744 | tf_op jit(solution)/shard_map/ppermute | solution.py:76
  26.1 14.1 %collective-permute-start.12 = (bf16[64,1152]{1,0:T(8,128)(2,1)S(1)}, bf16[64,1152]{1,0:T(8,128)(2,1)S(1)}, u32[]{:S(2)}, u32[]{:S(2)}) collective-permute-start(bf16[64,1152]{1,0:T(8,128)(2,1)S(1)} %pad_maximum_fusion.9), channel_id=1, source_target_pairs={{0,24},{1,25},{2,26},{3,27},{4,28},{5,29},{6,30},{7,31},{8,16},{9,... | collective-permute-start | bytes 442376 | tf_op jit(solution)/shard_map/ppermute | solution.py:76
  32.9 8.8 %collective-permute-start.8 = (bf16[192,1024]{1,0:T(8,128)(2,1)S(1)}, bf16[192,1024]{1,0:T(8,128)(2,1)S(1)}, u32[]{:S(2)}, u32[]{:S(2)}) collective-permute-start(bf16[192,1024]{1,0:T(8,128)(2,1)S(1)} %pad_maximum_fusion.3), channel_id=1, source_target_pairs={{0,4},{1,5},{2,6},{3,7},{4,0},{5,1},{6,2},{7,3},{8,12},{9,13},{10,... | collective-permute-start | bytes 1179656 | tf_op jit(solution)/shard_map/ppermute | solution.py:76
  34.6 9.4 %collective-permute-start.18 = (bf16[192,1024]{1,0:T(8,128)(2,1)S(1)}, bf16[192,1024]{1,0:T(8,128)(2,1)S(1)}, u32[]{:S(2)}, u32[]{:S(2)}) collective-permute-start(bf16[192,1024]{1,0:T(8,128)(2,1)S(1)} %pad_maximum_fusion.4), channel_id=1, source_target_pairs={{0,4},{1,5},{2,6},{3,7},{4,0},{5,1},{6,2},{7,3},{8,12},{9,13},{10,... | collective-permute-start | bytes 1179656 | tf_op jit(solution)/shard_map/ppermute | solution.py:76
  48.4 13.8 %collective-permute-start.21 = (bf16[128,1024]{1,0:T(8,128)(2,1)S(1)}, bf16[128,1024]{1,0:T(8,128)(2,1)S(1)}, u32[]{:S(2)}, u32[]{:S(2)}) collective-permute-start(bf16[128,1024]{1,0:T(8,128)(2,1)S(1)} %add_convert_fusion.3), channel_id=1, source_target_pairs={{0,8},{1,9},{2,10},{3,11},{4,20},{5,21},{6,22},{7,23},{8,0},{9,1},... | collective-permute-start | bytes 786440 | tf_op jit(solution)/shard_map/ppermute | solution.py:76
  49.5 13.3 %collective-permute-start.25 = (bf16[128,1024]{1,0:T(8,128)(2,1)S(1)}, bf16[128,1024]{1,0:T(8,128)(2,1)S(1)}, u32[]{:S(2)}, u32[]{:S(2)}) collective-permute-start(bf16[128,1024]{1,0:T(8,128)(2,1)S(1)} %slice.141), channel_id=1, source_target_pairs={{0,8},{1,9},{2,10},{3,11},{4,20},{5,21},{6,22},{7,23},{8,0},{9,1},... | collective-permute-start | bytes 786440 | tf_op jit(solution)/shard_map/ppermute | solution.py:76
  51.5 10.4 %collective-permute-start.29 = (bf16[128,1024]{1,0:T(8,128)(2,1)S(1)}, bf16[128,1024]{1,0:T(8,128)(2,1)S(1)}, u32[]{:S(2)}, u32[]{:S(2)}) collective-permute-start(bf16[128,1024]{1,0:T(8,128)(2,1)S(1)} %slice.146), channel_id=1, source_target_pairs={{0,8},{1,9},{2,10},{3,11},{4,20},{5,21},{6,22},{7,23},{8,0},{9,1},... | collective-permute-start | bytes 786440 | tf_op jit(solution)/shard_map/ppermute | solution.py:76
  52.6 12.7 %collective-permute-start.35 = (bf16[128,1024]{1,0:T(8,128)(2,1)S(1)}, bf16[128,1024]{1,0:T(8,128)(2,1)S(1)}, u32[]{:S(2)}, u32[]{:S(2)}) collective-permute-start(bf16[128,1024]{1,0:T(8,128)(2,1)S(1)} %slice.151), channel_id=1, source_target_pairs={{0,8},{1,9},{2,10},{3,11},{4,20},{5,21},{6,22},{7,23},{8,0},{9,1},... | collective-permute-start | bytes 786440 | tf_op jit(solution)/shard_map/ppermute | solution.py:76
  54.2 11.8 %collective-permute-start.28 = (bf16[64,1024]{1,0:T(8,128)(2,1)S(1)}, bf16[64,1024]{1,0:T(8,128)(2,1)S(1)}, u32[]{:S(2)}, u32[]{:S(2)}) collective-permute-start(bf16[64,1024]{1,0:T(8,128)(2,1)S(1)} %slice.145), channel_id=1, source_target_pairs={{0,24},{1,25},{2,26},{3,27},{4,28},{5,29},{6,30},{7,31},{8,16},{9,... | collective-permute-start | bytes 393224 | tf_op jit(solution)/shard_map/ppermute | solution.py:76
  62.3 26.4 %collective-permute-start.20 = (bf16[64,1024]{1,0:T(8,128)(2,1)S(1)}, bf16[64,1024]{1,0:T(8,128)(2,1)S(1)}, u32[]{:S(2)}, u32[]{:S(2)}) collective-permute-start(bf16[64,1024]{1,0:T(8,128)(2,1)S(1)} %add_convert_fusion.8), channel_id=1, source_target_pairs={{0,24},{1,25},{2,26},{3,27},{4,28},{5,29},{6,30},{7,31},{8,16},{9,... | collective-permute-start | bytes 393224 | tf_op jit(solution)/shard_map/ppermute | solution.py:76
  62.8 15.5 %collective-permute-start.24 = (bf16[64,1024]{1,0:T(8,128)(2,1)S(1)}, bf16[64,1024]{1,0:T(8,128)(2,1)S(1)}, u32[]{:S(2)}, u32[]{:S(2)}) collective-permute-start(bf16[64,1024]{1,0:T(8,128)(2,1)S(1)} %slice.140), channel_id=1, source_target_pairs={{0,24},{1,25},{2,26},{3,27},{4,28},{5,29},{6,30},{7,31},{8,16},{9,... | collective-permute-start | bytes 393224 | tf_op jit(solution)/shard_map/ppermute | solution.py:76
  65.4 9.4 %collective-permute-start.34 = (bf16[64,1024]{1,0:T(8,128)(2,1)S(1)}, bf16[64,1024]{1,0:T(8,128)(2,1)S(1)}, u32[]{:S(2)}, u32[]{:S(2)}) collective-permute-start(bf16[64,1024]{1,0:T(8,128)(2,1)S(1)} %slice.150), channel_id=1, source_target_pairs={{0,24},{1,25},{2,26},{3,27},{4,28},{5,29},{6,30},{7,31},{8,16},{9,... | collective-permute-start | bytes 393224 | tf_op jit(solution)/shard_map/ppermute | solution.py:76
  66.1 22.6 %collective-permute-start.22 = (bf16[64,1024]{1,0:T(8,128)(2,1)S(1)}, bf16[64,1024]{1,0:T(8,128)(2,1)S(1)}, u32[]{:S(2)}, u32[]{:S(2)}) collective-permute-start(bf16[64,1024]{1,0:T(8,128)(2,1)S(1)} %slice.138), channel_id=1, source_target_pairs={{0,4},{1,5},{2,6},{3,7},{4,0},{5,1},{6,2},{7,3},{8,12},{9,13},{10,... | collective-permute-start | bytes 393224 | tf_op jit(solution)/shard_map/ppermute | solution.py:76
  74.8 13.5 %collective-permute-start.31 = (bf16[64,1024]{1,0:T(8,128)(2,1)S(1)}, bf16[64,1024]{1,0:T(8,128)(2,1)S(1)}, u32[]{:S(2)}, u32[]{:S(2)}) collective-permute-start(bf16[64,1024]{1,0:T(8,128)(2,1)S(1)} %add_convert_fusion.7), channel_id=1, source_target_pairs={{0,2},{1,3},{2,0},{3,1},{4,6},{5,7},{6,4},{7,5},{8,10},{9,11},{10,... | collective-permute-start | bytes 393224 | tf_op jit(solution)/shard_map/ppermute | solution.py:76
  78.3 12.5 %collective-permute-start.37 = (bf16[64,1024]{1,0:T(8,128)(2,1)S(1)}, bf16[64,1024]{1,0:T(8,128)(2,1)S(1)}, u32[]{:S(2)}, u32[]{:S(2)}) collective-permute-start(bf16[64,1024]{1,0:T(8,128)(2,1)S(1)} %add_convert_fusion.5), channel_id=1, source_target_pairs={{0,2},{1,3},{2,0},{3,1},{4,6},{5,7},{6,4},{7,5},{8,10},{9,11},{10,... | collective-permute-start | bytes 393224 | tf_op jit(solution)/shard_map/ppermute | solution.py:76
  (15 other events, 65.8 us)

commit v5 on v4

--- a/solution.py
+++ b/solution.py
@@ -6,11 +6,13 @@
 from jax.sharding import PartitionSpec as P
 
 
-IN_CHUNKS = [[0], [1], [2], [3]]
+IN_CHUNKS = [[0], [2], [1], [3]]
 OUT_CHUNKS = [[3], [2], [1], [0]]
-TERMS_IN = 2
-SPLIT = (3,)
-IN_DIRECT = (0, 1, 2, 3)
+TERMS_IN = 1
+LEND_IN = 1
+LEND_OUT = 1
+SPLIT = (1, 3)
+IN_DIRECT = (0, 1, 3)
 OUT_DIRECT = (0, 1, 2, 3)
 
 
@@ -189,14 +191,22 @@
     places = mz ^ jnp.arange(shards, dtype=jnp.int32)
     pairs = load_slices(places, [w_gate, w_up], 1, 2 << 20)
     downs = load_slices(places, [w_down], 2, 2 << 20)
-    zs = {k: along(tokens, k) for k in range(1, shards)}
+    zs = {k: along(tokens, k) for k in range(1 + LEND_IN, shards)}
     acc = [0.0, 0.0]
     weight = None
     for n, ks in enumerate(IN_CHUNKS):
-        parts = [tokens if k == 0 else zs[k] for k in ks]
+        parts = [tokens if k == 0 else zs.get(k) for k in ks]
         if n == TERMS_IN:
             parts.append(terms)
-        both = spread(jnp.concatenate(parts, axis=1) if len(parts) > 1 else parts[0], str(n))
+        if ks == [1] and LEND_IN:
+            mine = along(first, 1)
+            both = mine, core_pair(mine)
+        else:
+            both = spread(
+                jnp.concatenate(parts, axis=1) if len(parts) > 1 else parts[0], str(n)
+            )
+        if n == 0:
+            first = both[0]
         for i, k in enumerate(ks):
             for h in range(2):
                 acc[h] = acc[h] + jnp.dot(
@@ -214,7 +224,7 @@
     hidden = [
         half(jax.nn.silu(a[:, :units]) * a[:, units:] * w[:, None]) for a, w in zip(acc, weight)
     ]
-    sums, passed = {}, {}
+    sums, lent = {}, []
     for n, ks in enumerate(OUT_CHUNKS):
         def product(h, start, stop):
             return jnp.concatenate(
@@ -224,18 +234,19 @@
                 axis=1,
             )
 
-        total = collect(lambda *rows: product(0, *rows), lambda *rows: product(1, *rows), str(n))
+        if ks == [1] and LEND_OUT:
+            got = core_pair(half(product(1, 0, None)))
+            part = half(product(0, 0, None) + f32(got))
+            lent.append(along(part, 1))
+            continue
+        total = collect(lambda *rows: product(0, *rows) + sum(f32(v[slice(*rows)]) for v in lent if ks == [0]), lambda *rows: product(1, *rows), str(n))
         for i, k in enumerate(ks):
             sums[k] = total[:, i * cols : (i + 1) * cols]
-            if k ^ 2 in passed:
-                sums[k] = sums[k] + f32(passed[k ^ 2])
             if k:
                 sums[k] = half(sums[k])
-            if k > 2:
-                passed[k] = along(sums[k], 2)
     mixed = sums[0]
     for k in range(1, shards):
-        if k not in passed:
+        if k in sums:
             mixed = mixed + f32(along(sums[k], k))
     return half(mixed)
 
@@ -244,7 +255,7 @@
     tok_rows, top_count = args[1].shape
     experts, shards = lax.axis_size("expert"), lax.axis_size("tensor")
     capacity = min(tok_rows, 3 * tok_rows * top_count // (2 * experts))
-    if capacity == tok_rows and experts == 1 << 3 and shards & (shards - 1) == 0 and shards > 2:
+    if capacity == tok_rows and experts == 1 << 3 and shards == len(IN_CHUNKS):
         return gather_plan(*args)
     return slot_plan(*args)
 

time: 94.6 us -> 81.1 us (0.86)
  waiting for transfers between devices: 45.3 us -> 25.4 us
  starting transfers between devices: 31.5 us -> 37.6 us
    ppermute x38 -> x32, waiting for transfers between devices: 45.3 us -> 25.4 us  [toward(): return lax.ppermute(a, ('expert', 'tensor'), pairs)]
    ppermute x38 -> x32, starting transfers between devices: 31.5 us -> 37.6 us  [toward(): return lax.ppermute(a, ('expert', 'tensor'), pairs)]
    dot_general x10 -> x12, matrix products: 3.91 us -> 4.27 us  [product(): jnp.dot(hidden[h][start:stop], downs[k], preferred_element_type=jnp.float32)]
  transfers between devices with their start and end apart: 38 -> 32, of which waited for: 12 -> 10; matrix products, arithmetic and copies ran while one was open for 10% -> 12% of each run, Pallas kernels for 6% -> 7%
where the time goes in v5:
time: 81.1 us; the launch traced here: 80.9 us
  starting transfers between devices  37.6 us (46%)
  waiting for transfers between devices  25.4 us (31%)
  matrix products  8.83 us (11%)
  Pallas kernels  5.84 us (7%)
  other arithmetic  2.49 us (3%)
    ppermute x32, starting transfers between devices, toward(): return lax.ppermute(a, ('expert', 'tensor'), pairs)  37.6 us
    ppermute x32, waiting for transfers between devices, toward(): return lax.ppermute(a, ('expert', 'tensor'), pairs)  25.4 us
    pallas_call x2, Pallas kernels, load_slices(): pl.pallas_call(kernel, out_shape=[out] * count, in_specs=[pl.BlockSpec(me...  5.84 us
    dot_general x8, matrix products, gather_plan(): jnp.dot(both[h][:, i * cols:(i + 1) * cols], pairs[k], preferred_element_...  4.56 us
    dot_general x12, matrix products, product(): jnp.dot(hidden[h][start:stop], downs[k], preferred_element_type=jnp.float32)  4.27 us
  transfers between devices with their start and end apart: 32, of which 10 were waited for; matrix products, arithmetic and copies ran while one was open for 12% of the time, Pallas kernels for 7%

profile of v5, /device:TPU:0, one launch (start us, length us, event | category | flops | bytes accessed | tf_op | source)
XLA Modules:
  0.0 80.9 jit_solution(4904251768083159220)
XLA Ops:
  0.5 3.4 %collective-permute-start.2 = (bf16[64,1024]{1,0:T(8,128)(2,1)}, bf16[64,1024]{1,0:T(8,128)(2,1)S(1)}, u32[]{:S(2)}, u32[]{:S(2)}) collective-permute-start(bf16[64,1024]{1,0:T(8,128)(2,1)} %param.6), channel_id=1, source_target_pairs={{0,24},{1,25},{2,26},{3,27},{4,28},{5,29},{6,30},{7,31},{8,16},{9,... | collective-permute-start | bytes 393224 | tf_op jit(solution)/shard_map/ppermute | solution.py:78
  3.9 2.6 %collective-permute-start.4 = (bf16[64,1024]{1,0:T(8,128)(2,1)}, bf16[64,1024]{1,0:T(8,128)(2,1)S(1)}, u32[]{:S(2)}, u32[]{:S(2)}) collective-permute-start(bf16[64,1024]{1,0:T(8,128)(2,1)} %param.6), channel_id=1, source_target_pairs={{0,2},{1,3},{2,0},{3,1},{4,6},{5,7},{6,4},{7,5},{8,10},{9,11},{10,... | collective-permute-start | bytes 393224 | tf_op jit(solution)/shard_map/ppermute | solution.py:78
  6.5 1.3 %collective-permute-start.11 = (bf16[64,1024]{1,0:T(8,128)(2,1)}, bf16[64,1024]{1,0:T(8,128)(2,1)S(1)}, u32[]{:S(2)}, u32[]{:S(2)}) collective-permute-start(bf16[64,1024]{1,0:T(8,128)(2,1)} %param.6), channel_id=1, source_target_pairs={{0,3},{1,2},{2,1},{3,0},{4,7},{5,6},{6,5},{7,4},{8,11},{9,10},{10,... | collective-permute-start | bytes 393224 | tf_op jit(solution)/shard_map/ppermute | solution.py:78
  7.9 0.7 select_reduce_fusion.2
  8.7 2.4 %shard_map.65 = (bf16[384,1024]{1,0:T(8,128)(2,1)S(1)}, bf16[384,1024]{1,0:T(8,128)(2,1)S(1)}, bf16[384,1024]{1,0:T(8,128)(2,1)S(1)}, bf16[384,1024]{1,0:T(8,128)(2,1)S(1)}) custom-call(s32[4]{0:T(128)S(1)} %iota_xor_fusion.places_ref, bf16[1,384,4096]{2,1,0:T(8,128)(2,1)} %refs_0_.3), custom_call_target="tpu_custom_call" | custom-call | tf_op jit(solution)/shard_map/pallas_call | solution.py:130
  11.2 3.4 %shard_map.64 = (bf16[1024,768]{1,0:T(8,128)(2,1)S(1)}, bf16[1024,768]{1,0:T(8,128)(2,1)S(1)}, bf16[1024,768]{1,0:T(8,128)(2,1)S(1)}, bf16[1024,768]{1,0:T(8,128)(2,1)S(1)}) custom-call(s32[4]{0:T(128)S(1)} %iota_xor_fusion.places_ref, bf16[1,4096,384]{2,1,0:T(8,128)(2,1)} %refs_0_.2, bf16[1,4096,384]{2,1,0:T(8,128)(2,1)} %refs_1_.1), custom_call_target="tpu_custom_call" | custom-call | tf_op jit(solution)/shard_map/pallas_call | solution.py:130
  14.7 2.3 %collective-permute-done.4 = bf16[64,1024]{1,0:T(8,128)(2,1)S(1)} collective-permute-done((bf16[64,1024]{1,0:T(8,128)(2,1)}, bf16[64,1024]{1,0:T(8,128)(2,1)S(1)}, u32[]{:S(2)}, u32[]{:S(2)}) %collective-permute-start.4) | collective-permute-done | bytes 131104 | tf_op jit(solution)/shard_map/ppermute | solution.py:78
  17.3 1.9 %collective-permute-start.1 = (bf16[128,1024]{1,0:T(8,128)(2,1)S(1)}, bf16[128,1024]{1,0:T(8,128)(2,1)S(1)}, u32[]{:S(2)}, u32[]{:S(2)}) collective-permute-start(bf16[128,1024]{1,0:T(8,128)(2,1)S(1)} %pad_maximum_fusion.5), channel_id=1, source_target_pairs={{0,8},{1,9},{2,10},{3,11},{4,20},{5,21},{6,22},{7,23},{8,0},{9,1},... | collective-permute-start | bytes 786440 | tf_op jit(solution)/shard_map/ppermute | solution.py:78
  19.2 1.5 %collective-permute-start.14 = (bf16[64,1024]{1,0:T(8,128)(2,1)S(1)}, bf16[64,1024]{1,0:T(8,128)(2,1)S(1)}, u32[]{:S(2)}, u32[]{:S(2)}) collective-permute-start(bf16[64,1024]{1,0:T(8,128)(2,1)S(1)} %collective-permute-done.11), channel_id=1, source_target_pairs={{0,24},{1,25},{2,26},{3,27},{4,28},{5,29},{6,30},{7,31},{8,16},{9,... | collective-permute-start | bytes 393224 | tf_op jit(solution)/shard_map/ppermute | solution.py:78
  20.7 1.6 %collective-permute-start.13 = (bf16[128,1024]{1,0:T(8,128)(2,1)S(1)}, bf16[128,1024]{1,0:T(8,128)(2,1)S(1)}, u32[]{:S(2)}, u32[]{:S(2)}) collective-permute-start(bf16[128,1024]{1,0:T(8,128)(2,1)S(1)} %pad_maximum_fusion.6), channel_id=1, source_target_pairs={{0,8},{1,9},{2,10},{3,11},{4,20},{5,21},{6,22},{7,23},{8,0},{9,1},... | collective-permute-start | bytes 786440 | tf_op jit(solution)/shard_map/ppermute | solution.py:78
  22.3 4.1 %collective-permute-done.1 = bf16[128,1024]{1,0:T(8,128)(2,1)S(1)} collective-permute-done((bf16[128,1024]{1,0:T(8,128)(2,1)S(1)}, bf16[128,1024]{1,0:T(8,128)(2,1)S(1)}, u32[]{:S(2)}, u32[]{:S(2)}) %collective-permute-start.1) | collective-permute-done | bytes 262176 | tf_op jit(solution)/shard_map/ppermute | solution.py:78
  27.0 4.1 %collective-permute-start.9 = (bf16[256,1024]{1,0:T(8,128)(2,1)S(1)}, bf16[256,1024]{1,0:T(8,128)(2,1)S(1)}, u32[]{:S(2)}, u32[]{:S(2)}) collective-permute-start(bf16[256,1024]{1,0:T(8,128)(2,1)S(1)} %constant_dynamic-update-slice_fusion), channel_id=1, source_target_pairs={{0,1},{1,0},{2,3},{3,2},{4,5},{5,4},{6,7},{7,6},{8,9},{9,8},{10,11... | collective-permute-start | bytes 1572872 | tf_op jit(solution)/shard_map/ppermute | solution.py:78
  32.4 1.5 %collective-permute-done.6 = bf16[128,1152]{1,0:T(8,128)(2,1)S(1)} collective-permute-done((bf16[128,1152]{1,0:T(8,128)(2,1)S(1)}, bf16[128,1152]{1,0:T(8,128)(2,1)S(1)}, u32[]{:S(2)}, u32[]{:S(2)}) %collective-permute-start.6) | collective-permute-done | bytes 294944 | tf_op jit(solution)/shard_map/ppermute | solution.py:78
  35.5 8.3 %collective-permute-done.9 = bf16[256,1024]{1,0:T(8,128)(2,1)S(1)} collective-permute-done((bf16[256,1024]{1,0:T(8,128)(2,1)S(1)}, bf16[256,1024]{1,0:T(8,128)(2,1)S(1)}, u32[]{:S(2)}, u32[]{:S(2)}) %collective-permute-start.9) | collective-permute-done | bytes 524320 | tf_op jit(solution)/shard_map/ppermute | solution.py:78
  52.3 1.5 %collective-permute-start.24 = (bf16[128,1024]{1,0:T(8,128)(2,1)S(1)}, bf16[128,1024]{1,0:T(8,128)(2,1)S(1)}, u32[]{:S(2)}, u32[]{:S(2)}) collective-permute-start(bf16[128,1024]{1,0:T(8,128)(2,1)S(1)} %add_convert_fusion.2), channel_id=1, source_target_pairs={{0,8},{1,9},{2,10},{3,11},{4,20},{5,21},{6,22},{7,23},{8,0},{9,1},... | collective-permute-start | bytes 786440 | tf_op jit(solution)/shard_map/ppermute | solution.py:78
  54.2 1.9 %collective-permute-start.17 = (bf16[256,1024]{1,0:T(8,128)(2,1)S(1)}, bf16[256,1024]{1,0:T(8,128)(2,1)S(1)}, u32[]{:S(2)}, u32[]{:S(2)}) collective-permute-start(bf16[256,1024]{1,0:T(8,128)(2,1)S(1)} %add_convert_fusion.1), channel_id=1, source_target_pairs={{0,1},{1,0},{2,3},{3,2},{4,5},{5,4},{6,7},{7,6},{8,9},{9,8},{10,11... | collective-permute-start | bytes 1572872 | tf_op jit(solution)/shard_map/ppermute | solution.py:78
  56.4 1.3 %collective-permute-start.28 = (bf16[64,1024]{1,0:T(8,128)(2,1)S(1)}, bf16[64,1024]{1,0:T(8,128)(2,1)S(1)}, u32[]{:S(2)}, u32[]{:S(2)}) collective-permute-start(bf16[64,1024]{1,0:T(8,128)(2,1)S(1)} %slice.143), channel_id=1, source_target_pairs={{0,24},{1,25},{2,26},{3,27},{4,28},{5,29},{6,30},{7,31},{8,16},{9,... | collective-permute-start | bytes 393224 | tf_op jit(solution)/shard_map/ppermute | solution.py:78
  58.1 3.9 %collective-permute-done.24 = bf16[128,1024]{1,0:T(8,128)(2,1)S(1)} collective-permute-done((bf16[128,1024]{1,0:T(8,128)(2,1)S(1)}, bf16[128,1024]{1,0:T(8,128)(2,1)S(1)}, u32[]{:S(2)}, u32[]{:S(2)}) %collective-permute-start.24) | collective-permute-done | bytes 262176 | tf_op jit(solution)/shard_map/ppermute | solution.py:78
  61.9 1.3 %collective-permute-start.23 = (bf16[64,1024]{1,0:T(8,128)(2,1)S(1)}, bf16[64,1024]{1,0:T(8,128)(2,1)S(1)}, u32[]{:S(2)}, u32[]{:S(2)}) collective-permute-start(bf16[64,1024]{1,0:T(8,128)(2,1)S(1)} %add_convert_fusion.7), channel_id=1, source_target_pairs={{0,24},{1,25},{2,26},{3,27},{4,28},{5,29},{6,30},{7,31},{8,16},{9,... | collective-permute-start | bytes 393224 | tf_op jit(solution)/shard_map/ppermute | solution.py:78
  63.9 3.3 %collective-permute-start.31 = (bf16[64,1024]{1,0:T(8,128)(2,1)S(1)}, bf16[64,1024]{1,0:T(8,128)(2,1)S(1)}, u32[]{:S(2)}, u32[]{:S(2)}) collective-permute-start(bf16[64,1024]{1,0:T(8,128)(2,1)S(1)} %add_convert_fusion.5), channel_id=1, source_target_pairs={{0,3},{1,2},{2,1},{3,0},{4,7},{5,6},{6,5},{7,4},{8,11},{9,10},{10,... | collective-permute-start | bytes 393224 | tf_op jit(solution)/shard_map/ppermute | solution.py:78
  68.8 5.0 %collective-permute-start.26 = (bf16[64,1024]{1,0:T(8,128)(2,1)S(1)}, bf16[64,1024]{1,0:T(8,128)(2,1)S(1)}, u32[]{:S(2)}, u32[]{:S(2)}) collective-permute-start(bf16[64,1024]{1,0:T(8,128)(2,1)S(1)} %add_convert_fusion.6), channel_id=1, source_target_pairs={{0,2},{1,3},{2,0},{3,1},{4,6},{5,7},{6,4},{7,5},{8,10},{9,11},{10,... | collective-permute-start | bytes 393224 | tf_op jit(solution)/shard_map/ppermute | solution.py:78
  74.0 1.9 %collective-permute-start.19 = (bf16[64,1024]{1,0:T(8,128)(2,1)S(1)}, bf16[64,1024]{1,0:T(8,128)(2,1)S(1)}, u32[]{:S(2)}, u32[]{:S(2)}) collective-permute-start(bf16[64,1024]{1,0:T(8,128)(2,1)S(1)} %add_convert_fusion.8), channel_id=1, source_target_pairs={{0,24},{1,25},{2,26},{3,27},{4,28},{5,29},{6,30},{7,31},{8,16},{9,... | collective-permute-start | bytes 393224 | tf_op jit(solution)/shard_map/ppermute | solution.py:78
  76.3 3.7 %collective-permute-done.26 = bf16[64,1024]{1,0:T(8,128)(2,1)S(1)} collective-permute-done((bf16[64,1024]{1,0:T(8,128)(2,1)S(1)}, bf16[64,1024]{1,0:T(8,128)(2,1)S(1)}, u32[]{:S(2)}, u32[]{:S(2)}) %collective-permute-start.26) | collective-permute-done | bytes 131104 | tf_op jit(solution)/shard_map/ppermute | solution.py:78
  80.1 0.8 %add_convert_fusion.4 = bf16[64,1024]{1,0:T(8,128)(2,1)} fusion(bf16[64,1024]{1,0:T(8,128)(2,1)S(1)} %collective-permute-done.31, bf16[64,1024]{1,0:T(8,128)(2,1)S(1)} %collective-permute-done.26, bf16[64,1024]{1,0:T(8,128)(2,1)S(1)} %collective-permute-done.21, bf16[64,1024]{1,0:T(8,128)(2,1)S(1)} %collective-permute-done.19, f32[64,1024]{1,0:T(8,128)S(1)} %fusion.34, ...), kind=kLoop, calls=%fused_computation.37 | loop fusion | flops 983040 | bytes 1310720 | tf_op jit(solution)/shard_map/convert_element_type | solution.py:106
  (97 shorter events, 16.8 us)
Async XLA Ops:
  0.0 17.3 %collective-permute-start = (bf16[64,1024]{1,0:T(8,128)(2,1)}, bf16[64,1024]{1,0:T(8,128)(2,1)S(1)}, u32[]{:S(2)}, u32[]{:S(2)}) collective-permute-start(bf16[64,1024]{1,0:T(8,128)(2,1)} %param.6), channel_id=1, source_target_pairs={{0,4},{1,5},{2,6},{3,7},{4,0},{5,1},{6,2},{7,3},{8,12},{9,13},{10,... | collective-permute-start | bytes 393224 | tf_op jit(solution)/shard_map/ppermute | solution.py:78
  0.5 26.5 %collective-permute-start.2 = (bf16[64,1024]{1,0:T(8,128)(2,1)}, bf16[64,1024]{1,0:T(8,128)(2,1)S(1)}, u32[]{:S(2)}, u32[]{:S(2)}) collective-permute-start(bf16[64,1024]{1,0:T(8,128)(2,1)} %param.6), channel_id=1, source_target_pairs={{0,24},{1,25},{2,26},{3,27},{4,28},{5,29},{6,30},{7,31},{8,16},{9,... | collective-permute-start | bytes 393224 | tf_op jit(solution)/shard_map/ppermute | solution.py:78
  3.9 13.1 %collective-permute-start.4 = (bf16[64,1024]{1,0:T(8,128)(2,1)}, bf16[64,1024]{1,0:T(8,128)(2,1)S(1)}, u32[]{:S(2)}, u32[]{:S(2)}) collective-permute-start(bf16[64,1024]{1,0:T(8,128)(2,1)} %param.6), channel_id=1, source_target_pairs={{0,2},{1,3},{2,0},{3,1},{4,6},{5,7},{6,4},{7,5},{8,10},{9,11},{10,... | collective-permute-start | bytes 393224 | tf_op jit(solution)/shard_map/ppermute | solution.py:78
  6.5 8.1 %collective-permute-start.11 = (bf16[64,1024]{1,0:T(8,128)(2,1)}, bf16[64,1024]{1,0:T(8,128)(2,1)S(1)}, u32[]{:S(2)}, u32[]{:S(2)}) collective-permute-start(bf16[64,1024]{1,0:T(8,128)(2,1)} %param.6), channel_id=1, source_target_pairs={{0,3},{1,2},{2,1},{3,0},{4,7},{5,6},{6,5},{7,4},{8,11},{9,10},{10,... | collective-permute-start | bytes 393224 | tf_op jit(solution)/shard_map/ppermute | solution.py:78
  17.0 15.3 %collective-permute-start.7 = (bf16[64,1152]{1,0:T(8,128)(2,1)S(1)}, bf16[64,1152]{1,0:T(8,128)(2,1)S(1)}, u32[]{:S(2)}, u32[]{:S(2)}) collective-permute-start(bf16[64,1152]{1,0:T(8,128)(2,1)S(1)} %pad_maximum_fusion.7), channel_id=1, source_target_pairs={{0,24},{1,25},{2,26},{3,27},{4,28},{5,29},{6,30},{7,31},{8,16},{9,... | collective-permute-start | bytes 442376 | tf_op jit(solution)/shard_map/ppermute | solution.py:78
  17.3 9.1 %collective-permute-start.1 = (bf16[128,1024]{1,0:T(8,128)(2,1)S(1)}, bf16[128,1024]{1,0:T(8,128)(2,1)S(1)}, u32[]{:S(2)}, u32[]{:S(2)}) collective-permute-start(bf16[128,1024]{1,0:T(8,128)(2,1)S(1)} %pad_maximum_fusion.5), channel_id=1, source_target_pairs={{0,8},{1,9},{2,10},{3,11},{4,20},{5,21},{6,22},{7,23},{8,0},{9,1},... | collective-permute-start | bytes 786440 | tf_op jit(solution)/shard_map/ppermute | solution.py:78
  19.2 12.5 %collective-permute-start.14 = (bf16[64,1024]{1,0:T(8,128)(2,1)S(1)}, bf16[64,1024]{1,0:T(8,128)(2,1)S(1)}, u32[]{:S(2)}, u32[]{:S(2)}) collective-permute-start(bf16[64,1024]{1,0:T(8,128)(2,1)S(1)} %collective-permute-done.11), channel_id=1, source_target_pairs={{0,24},{1,25},{2,26},{3,27},{4,28},{5,29},{6,30},{7,31},{8,16},{9,... | collective-permute-start | bytes 393224 | tf_op jit(solution)/shard_map/ppermute | solution.py:78
  20.7 11.5 %collective-permute-start.13 = (bf16[128,1024]{1,0:T(8,128)(2,1)S(1)}, bf16[128,1024]{1,0:T(8,128)(2,1)S(1)}, u32[]{:S(2)}, u32[]{:S(2)}) collective-permute-start(bf16[128,1024]{1,0:T(8,128)(2,1)S(1)} %pad_maximum_fusion.6), channel_id=1, source_target_pairs={{0,8},{1,9},{2,10},{3,11},{4,20},{5,21},{6,22},{7,23},{8,0},{9,1},... | collective-permute-start | bytes 786440 | tf_op jit(solution)/shard_map/ppermute | solution.py:78
  26.4 7.4 %collective-permute-start.6 = (bf16[128,1152]{1,0:T(8,128)(2,1)S(1)}, bf16[128,1152]{1,0:T(8,128)(2,1)S(1)}, u32[]{:S(2)}, u32[]{:S(2)}) collective-permute-start(bf16[128,1152]{1,0:T(8,128)(2,1)S(1)} %pad_maximum_fusion.4), channel_id=1, source_target_pairs={{0,8},{1,9},{2,10},{3,11},{4,20},{5,21},{6,22},{7,23},{8,0},{9,1},... | collective-permute-start | bytes 884744 | tf_op jit(solution)/shard_map/ppermute | solution.py:78
  27.0 16.8 %collective-permute-start.9 = (bf16[256,1024]{1,0:T(8,128)(2,1)S(1)}, bf16[256,1024]{1,0:T(8,128)(2,1)S(1)}, u32[]{:S(2)}, u32[]{:S(2)}) collective-permute-start(bf16[256,1024]{1,0:T(8,128)(2,1)S(1)} %constant_dynamic-update-slice_fusion), channel_id=1, source_target_pairs={{0,1},{1,0},{2,3},{3,2},{4,5},{5,4},{6,7},{7,6},{8,9},{9,8},{10,11... | collective-permute-start | bytes 1572872 | tf_op jit(solution)/shard_map/ppermute | solution.py:78
  32.2 14.6 %collective-permute-start.15 = (bf16[192,1024]{1,0:T(8,128)(2,1)S(1)}, bf16[192,1024]{1,0:T(8,128)(2,1)S(1)}, u32[]{:S(2)}, u32[]{:S(2)}) collective-permute-start(bf16[192,1024]{1,0:T(8,128)(2,1)S(1)} %pad_maximum_fusion.3), channel_id=1, source_target_pairs={{0,4},{1,5},{2,6},{3,7},{4,0},{5,1},{6,2},{7,3},{8,12},{9,13},{10,... | collective-permute-start | bytes 1179656 | tf_op jit(solution)/shard_map/ppermute | solution.py:78
  33.9 10.0 %collective-permute-start.8 = (bf16[192,1152]{1,0:T(8,128)(2,1)S(1)}, bf16[192,1152]{1,0:T(8,128)(2,1)S(1)}, u32[]{:S(2)}, u32[]{:S(2)}) collective-permute-start(bf16[192,1152]{1,0:T(8,128)(2,1)S(1)} %pad_maximum_fusion.1), channel_id=1, source_target_pairs={{0,4},{1,5},{2,6},{3,7},{4,0},{5,1},{6,2},{7,3},{8,12},{9,13},{10,... | collective-permute-start | bytes 1327112 | tf_op jit(solution)/shard_map/ppermute | solution.py:78
  49.6 17.6 %collective-permute-start.18 = (bf16[256,1024]{1,0:T(8,128)(2,1)S(1)}, bf16[256,1024]{1,0:T(8,128)(2,1)S(1)}, u32[]{:S(2)}, u32[]{:S(2)}) collective-permute-start(bf16[256,1024]{1,0:T(8,128)(2,1)S(1)} %convolution_convert_fusion.2), channel_id=1, source_target_pairs={{0,4},{1,5},{2,6},{3,7},{4,0},{5,1},{6,2},{7,3},{8,12},{9,13},{10,... | collective-permute-start | bytes 1572872 | tf_op jit(solution)/shard_map/ppermute | solution.py:78
  51.3 6.4 %collective-permute-start.29 = (bf16[128,1024]{1,0:T(8,128)(2,1)S(1)}, bf16[128,1024]{1,0:T(8,128)(2,1)S(1)}, u32[]{:S(2)}, u32[]{:S(2)}) collective-permute-start(bf16[128,1024]{1,0:T(8,128)(2,1)S(1)} %slice.144), channel_id=1, source_target_pairs={{0,8},{1,9},{2,10},{3,11},{4,20},{5,21},{6,22},{7,23},{8,0},{9,1},... | collective-permute-start | bytes 786440 | tf_op jit(solution)/shard_map/ppermute | solution.py:78
  52.3 9.7 %collective-permute-start.24 = (bf16[128,1024]{1,0:T(8,128)(2,1)S(1)}, bf16[128,1024]{1,0:T(8,128)(2,1)S(1)}, u32[]{:S(2)}, u32[]{:S(2)}) collective-permute-start(bf16[128,1024]{1,0:T(8,128)(2,1)S(1)} %add_convert_fusion.2), channel_id=1, source_target_pairs={{0,8},{1,9},{2,10},{3,11},{4,20},{5,21},{6,22},{7,23},{8,0},{9,1},... | collective-permute-start | bytes 786440 | tf_op jit(solution)/shard_map/ppermute | solution.py:78
  54.2 13.5 %collective-permute-start.17 = (bf16[256,1024]{1,0:T(8,128)(2,1)S(1)}, bf16[256,1024]{1,0:T(8,128)(2,1)S(1)}, u32[]{:S(2)}, u32[]{:S(2)}) collective-permute-start(bf16[256,1024]{1,0:T(8,128)(2,1)S(1)} %add_convert_fusion.1), channel_id=1, source_target_pairs={{0,1},{1,0},{2,3},{3,2},{4,5},{5,4},{6,7},{7,6},{8,9},{9,8},{10,11... | collective-permute-start | bytes 1572872 | tf_op jit(solution)/shard_map/ppermute | solution.py:78
  56.4 7.4 %collective-permute-start.28 = (bf16[64,1024]{1,0:T(8,128)(2,1)S(1)}, bf16[64,1024]{1,0:T(8,128)(2,1)S(1)}, u32[]{:S(2)}, u32[]{:S(2)}) collective-permute-start(bf16[64,1024]{1,0:T(8,128)(2,1)S(1)} %slice.143), channel_id=1, source_target_pairs={{0,24},{1,25},{2,26},{3,27},{4,28},{5,29},{6,30},{7,31},{8,16},{9,... | collective-permute-start | bytes 393224 | tf_op jit(solution)/shard_map/ppermute | solution.py:78
  57.7 6.1 %collective-permute-start.30 = (bf16[64,1024]{1,0:T(8,128)(2,1)S(1)}, bf16[64,1024]{1,0:T(8,128)(2,1)S(1)}, u32[]{:S(2)}, u32[]{:S(2)}) collective-permute-start(bf16[64,1024]{1,0:T(8,128)(2,1)S(1)} %slice.146), channel_id=1, source_target_pairs={{0,4},{1,5},{2,6},{3,7},{4,0},{5,1},{6,2},{7,3},{8,12},{9,13},{10,... | collective-permute-start | bytes 393224 | tf_op jit(solution)/shard_map/ppermute | solution.py:78
  61.9 6.7 %collective-permute-start.23 = (bf16[64,1024]{1,0:T(8,128)(2,1)S(1)}, bf16[64,1024]{1,0:T(8,128)(2,1)S(1)}, u32[]{:S(2)}, u32[]{:S(2)}) collective-permute-start(bf16[64,1024]{1,0:T(8,128)(2,1)S(1)} %add_convert_fusion.7), channel_id=1, source_target_pairs={{0,24},{1,25},{2,26},{3,27},{4,28},{5,29},{6,30},{7,31},{8,16},{9,... | collective-permute-start | bytes 393224 | tf_op jit(solution)/shard_map/ppermute | solution.py:78
  63.8 4.9 %collective-permute-start.25 = (bf16[64,1024]{1,0:T(8,128)(2,1)S(1)}, bf16[64,1024]{1,0:T(8,128)(2,1)S(1)}, u32[]{:S(2)}, u32[]{:S(2)}) collective-permute-start(bf16[64,1024]{1,0:T(8,128)(2,1)S(1)} %slice.141), channel_id=1, source_target_pairs={{0,4},{1,5},{2,6},{3,7},{4,0},{5,1},{6,2},{7,3},{8,12},{9,13},{10,... | collective-permute-start | bytes 393224 | tf_op jit(solution)/shard_map/ppermute | solution.py:78
  63.9 12.5 %collective-permute-start.31 = (bf16[64,1024]{1,0:T(8,128)(2,1)S(1)}, bf16[64,1024]{1,0:T(8,128)(2,1)S(1)}, u32[]{:S(2)}, u32[]{:S(2)}) collective-permute-start(bf16[64,1024]{1,0:T(8,128)(2,1)S(1)} %add_convert_fusion.5), channel_id=1, source_target_pairs={{0,3},{1,2},{2,1},{3,0},{4,7},{5,6},{6,5},{7,4},{8,11},{9,10},{10,... | collective-permute-start | bytes 393224 | tf_op jit(solution)/shard_map/ppermute | solution.py:78
  68.1 7.9 %collective-permute-start.20 = (bf16[128,1024]{1,0:T(8,128)(2,1)S(1)}, bf16[128,1024]{1,0:T(8,128)(2,1)S(1)}, u32[]{:S(2)}, u32[]{:S(2)}) collective-permute-start(bf16[128,1024]{1,0:T(8,128)(2,1)S(1)} %add_convert_fusion.3), channel_id=1, source_target_pairs={{0,8},{1,9},{2,10},{3,11},{4,20},{5,21},{6,22},{7,23},{8,0},{9,1},... | collective-permute-start | bytes 786440 | tf_op jit(solution)/shard_map/ppermute | solution.py:78
  68.8 11.3 %collective-permute-start.26 = (bf16[64,1024]{1,0:T(8,128)(2,1)S(1)}, bf16[64,1024]{1,0:T(8,128)(2,1)S(1)}, u32[]{:S(2)}, u32[]{:S(2)}) collective-permute-start(bf16[64,1024]{1,0:T(8,128)(2,1)S(1)} %add_convert_fusion.6), channel_id=1, source_target_pairs={{0,2},{1,3},{2,0},{3,1},{4,6},{5,7},{6,4},{7,5},{8,10},{9,11},{10,... | collective-permute-start | bytes 393224 | tf_op jit(solution)/shard_map/ppermute | solution.py:78
  74.0 6.0 %collective-permute-start.19 = (bf16[64,1024]{1,0:T(8,128)(2,1)S(1)}, bf16[64,1024]{1,0:T(8,128)(2,1)S(1)}, u32[]{:S(2)}, u32[]{:S(2)}) collective-permute-start(bf16[64,1024]{1,0:T(8,128)(2,1)S(1)} %add_convert_fusion.8), channel_id=1, source_target_pairs={{0,24},{1,25},{2,26},{3,27},{4,28},{5,29},{6,30},{7,31},{8,16},{9,... | collective-permute-start | bytes 393224 | tf_op jit(solution)/shard_map/ppermute | solution.py:78
  (9 other events, 30.1 us)
